TPU v7x, 32 devices: a whole 2x2x4 slice. The times are simulated.
32 devices in a mesh: section: 2 (over core), dp: 4 (over z), expert: 4 (over y, x).
Axes of the slice: x: 2, y: 2, z: 4, core: 2. Of those that a mesh axis runs over, the one named last changes fastest.
Arguments:
- boundary_in: float32 [2, 2, 16, 197, 768], P('section', None, ('dp', 'expert')), may hold values from -6 to 6
- routes: int32 [2, 2, 16, 197, 2], P('section', None, ('dp', 'expert')), may hold values from 0 to 7, as said below
- capacity_slots: int32 [2, 2, 16, 197, 2], P('section', None, ('dp', 'expert')), may hold values from 0 to 40, as said below
- ln_gain: bfloat16 [2, 2, 768], P('section', None, ('dp', 'expert')), may hold values from 0.5 to 1.5
- ln_bias: bfloat16 [2, 2, 768], P('section', None, ('dp', 'expert')), may hold values from -3 to 3
- w_qkv: bfloat16 [2, 768, 2304], P('section', ('dp', 'expert')), may hold values from -0.21875 to 0.21875
- w_out: bfloat16 [2, 768, 768], P('section', ('dp', 'expert')), may hold values from -1.25 to 1.25
- w_router: bfloat16 [2, 768, 8], P('section', ('dp', 'expert')), may hold values from -0.21875 to 0.21875
- w_up: bfloat16 [2, 8, 768, 3072], P('section', 'expert', None, 'dp'), may hold values from -0.21875 to 0.21875
- w_down: bfloat16 [2, 8, 3072, 768], P('section', 'expert', 'dp'), may hold values from -0.109375 to 0.109375
Outputs:
- boundary_out: float32 [2, 2, 16, 197, 768], P('section', None, ('dp', 'expert'))
- grad_ln_gain: float32 [2, 2, 768], P('section', None, ('dp', 'expert'))
- grad_ln_bias: float32 [2, 2, 768], P('section', None, ('dp', 'expert'))
- grad_qkv: float32 [2, 768, 2304], P('section', ('dp', 'expert'))
- grad_out: float32 [2, 768, 768], P('section', ('dp', 'expert'))
- grad_router: float32 [2, 768, 8], P('section', ('dp', 'expert'))
- grad_up: float32 [2, 8, 768, 3072], P('section', 'expert', None, 'dp')
- grad_down: float32 [2, 8, 3072, 768], P('section', 'expert', 'dp')
Inputs may be any that keep to these rules, and one draw needn't show every extreme that they name: `routes`: each token names two different experts of the 8. In every block (the 1 images of one micro-batch on one device of dp+expert, each layer apart) some expert is named by 40 or more tokens. `capacity_slots`: within a block, the kept choices of one expert hold the slots 0, 1, 2, ... without gaps or repeats; the value 40 marks a dropped choice, and every block drops at least one choice.
All inputs are finite; a program needn't handle non-finite values.
Results may differ from a plain program's by a relative error of at most 0.02.
Values may be sent and summed in bfloat16 or wider, within the bound.
A program may use at most 256 MiB of HBM per device.

v0:
```python
import math

import jax
import jax.numpy as jnp
from jax import lax
from jax.sharding import PartitionSpec as P

HEADS = 12
HEAD_DIM = 64
EXP_DEV = 2
MB = 2


EPS = 1e-06
SQRT_HALF = 0.7071067811865476
INV_ROOT_TAU = 0.3989422804014327


def shifted(x, axis, by):
    size = lax.axis_size(axis)
    pairs = [(i, i + by) for i in range(size) if 0 <= i + by < size]
    return lax.ppermute(x, axis, pairs)


def norm_forward(values, gain_row, shift_row):
    centred = values - jnp.mean(values, axis=-1, keepdims=True)
    variance = jnp.mean(centred * centred, axis=-1, keepdims=True)
    inverse = lax.rsqrt(variance + EPS)
    unit_rows = centred * inverse
    return (unit_rows * gain_row + shift_row, unit_rows, inverse)


def norm_backward(d_normed, unit_rows, inverse, gain_row):
    d_gain = jnp.sum(d_normed * unit_rows, axis=0)
    d_shift = jnp.sum(d_normed, axis=0)
    scaled = d_normed * gain_row
    d_values = inverse * (
        scaled
        - jnp.mean(scaled, axis=-1, keepdims=True)
        - unit_rows * jnp.mean(scaled * unit_rows, axis=-1, keepdims=True)
    )
    return (d_values, d_gain, d_shift)


def gelu_slope(pre_act):
    return (
        0.5 * (1.0 + lax.erf(pre_act * SQRT_HALF))
        + pre_act * jnp.exp(-0.5 * pre_act * pre_act) * INV_ROOT_TAU
    )


def split_heads(qkv_rows, image_count):
    feature_count = qkv_rows.shape[1] // 3
    return [
        qkv_rows[:, part_index * feature_count : (part_index + 1) * feature_count].reshape(
            image_count, -1, HEADS, HEAD_DIM
        )
        for part_index in range(3)
    ]


def attend_forward(qkv_rows, image_count):
    queries, key_rows, value_rows = split_heads(qkv_rows, image_count)
    scale_factor = 1.0 / math.sqrt(HEAD_DIM)
    scores = (
        jnp.einsum("bqhd,bkhd->bhqk", queries, key_rows, preferred_element_type=jnp.float32)
        * scale_factor
    )
    log_totals = jnp.log(jnp.sum(jnp.exp(scores), axis=-1))
    probs_half = jnp.exp(scores - log_totals[..., None]).astype(jnp.bfloat16)
    attended = jnp.einsum(
        "bhqk,bkhd->bqhd", probs_half, value_rows, preferred_element_type=jnp.float32
    )
    return (attended.astype(jnp.bfloat16).reshape(-1, HEADS * HEAD_DIM), log_totals)


def attend_backward(qkv_rows, log_totals, d_attended, image_count):
    queries, key_rows, value_rows = split_heads(qkv_rows, image_count)
    scale_factor = 1.0 / math.sqrt(HEAD_DIM)
    scores = (
        jnp.einsum("bqhd,bkhd->bhqk", queries, key_rows, preferred_element_type=jnp.float32)
        * scale_factor
    )
    probs = jnp.exp(scores - log_totals[..., None])
    probs_half = probs.astype(jnp.bfloat16)
    d_heads = d_attended.reshape(image_count, -1, HEADS, HEAD_DIM)
    d_values = jnp.einsum(
        "bhqk,bqhd->bkhd", probs_half, d_heads, preferred_element_type=jnp.float32
    )
    d_probs = jnp.einsum("bqhd,bkhd->bhqk", d_heads, value_rows, preferred_element_type=jnp.float32)
    row_dot = jnp.sum(probs * d_probs, axis=-1, keepdims=True)
    d_scores = (probs * (d_probs - row_dot) * scale_factor).astype(jnp.bfloat16)
    d_queries = jnp.einsum(
        "bhqk,bkhd->bqhd", d_scores, key_rows, preferred_element_type=jnp.float32
    )
    d_keys = jnp.einsum("bhqk,bqhd->bkhd", d_scores, queries, preferred_element_type=jnp.float32)
    feature_count = HEADS * HEAD_DIM
    joined = jnp.concatenate(
        [
            d_queries.reshape(-1, feature_count),
            d_keys.reshape(-1, feature_count),
            d_values.reshape(-1, feature_count),
        ],
        axis=1,
    )
    return joined.astype(jnp.bfloat16)


def on_device(
    boundary_in, routes, capacity_slots, ln_gain, ln_bias, w_qkv, w_out, w_router, w_up, w_down
):
    section_index = lax.axis_index("section")
    is_first = section_index == 0
    expert_count = EXP_DEV * lax.axis_size("expert")
    local_images = boundary_in.shape[2]
    token_rows = local_images * boundary_in.shape[3]
    model_width = boundary_in.shape[4]
    capacity = 26 * token_rows // (16 * expert_count)
    owned_rows = boundary_in[0].reshape(MB, token_rows, model_width)
    route_rows = routes[0].reshape(MB, token_rows, 2)
    slot_rows = capacity_slots[0].reshape(MB, token_rows, 2)
    dense_parts = (
        lax.all_gather(w_qkv, ("dp", "expert"), axis=1, tiled=True),
        lax.all_gather(w_out, ("dp", "expert"), axis=1, tiled=True),
        lax.all_gather(w_router, ("dp", "expert"), axis=1, tiled=True),
        lax.all_gather(ln_gain, ("dp", "expert"), axis=2, tiled=True),
        lax.all_gather(ln_bias, ("dp", "expert"), axis=2, tiled=True),
    )
    weight_qkv = dense_parts[0][0]
    weight_out = dense_parts[1][0]
    weight_router = dense_parts[2][0]
    gain_rows = dense_parts[3][0].astype(jnp.float32)
    shift_rows = dense_parts[4][0].astype(jnp.float32)
    weight_up = w_up[0]
    weight_down = w_down[0]

    def tables(expert_ids, slot_ids):
        slot_index = jnp.where(slot_ids < capacity, expert_ids * capacity + slot_ids, -1)
        columns = jnp.arange(expert_count * capacity, dtype=jnp.int32)
        onehot = (slot_index[:, :, None] == columns).astype(jnp.bfloat16)
        chosen = (expert_ids[:, :, None] == jnp.arange(expert_count, dtype=jnp.int32)).astype(
            jnp.float32
        )
        return (onehot, chosen)

    def forward_front(inputs, expert_ids, slot_ids):
        normed_one, unit_one, inverse_one = norm_forward(inputs, gain_rows[0], shift_rows[0])
        norm_one = normed_one.astype(jnp.bfloat16)
        qkv_rows = jnp.dot(norm_one, weight_qkv, preferred_element_type=jnp.float32).astype(
            jnp.bfloat16
        )
        attended, log_totals = attend_forward(qkv_rows, local_images)
        middle = inputs + jnp.dot(attended, weight_out, preferred_element_type=jnp.float32)
        normed_two, unit_two, inverse_two = norm_forward(middle, gain_rows[1], shift_rows[1])
        norm_two = normed_two.astype(jnp.bfloat16)
        logits = jnp.dot(norm_two, weight_router, preferred_element_type=jnp.float32)
        onehot, chosen = tables(expert_ids, slot_ids)
        picked = jnp.sum(logits[:, None, :] * chosen, axis=-1)
        leading = jax.nn.sigmoid(picked[:, 0] - picked[:, 1])
        gate_pair = jnp.stack([leading, 1.0 - leading], axis=-1)
        buffer = jnp.einsum(
            "tjs,td->sd", onehot, norm_two, preferred_element_type=jnp.float32
        ).astype(jnp.bfloat16)
        outbound = buffer.reshape(expert_count, capacity, model_width)
        return (norm_one, qkv_rows, log_totals, attended, middle, norm_two, gate_pair, outbound)

    def backward_front(d_out, gate_pair, back_rows, expert_ids, slot_ids):
        onehot, chosen = tables(expert_ids, slot_ids)
        selected = jnp.einsum("tjs,sd->tjd", onehot, back_rows, preferred_element_type=jnp.float32)
        d_gate = jnp.sum(d_out[:, None, :] * selected, axis=-1)
        d_lead = (d_gate[:, 0] - d_gate[:, 1]) * gate_pair[:, 0] * gate_pair[:, 1]
        d_logits = (d_lead[:, None] * (chosen[:, 0] - chosen[:, 1])).astype(jnp.bfloat16)
        weighted = gate_pair[:, :, None] * d_out[:, None, :]
        d_buffer = jnp.einsum(
            "tjs,tjd->sd", onehot.astype(jnp.float32), weighted, precision=lax.Precision.HIGHEST
        ).astype(jnp.bfloat16)
        return (d_logits, d_buffer.reshape(expert_count, capacity, model_width))

    def backward_finish(d_out, saved, d_back, d_logits, expert_ids, slot_ids):
        (
            inputs,
            norm_one,
            qkv_rows,
            log_totals,
            attended,
            middle,
            norm_two,
            gate_pair,
            back_rows,
            inbound,
            pre_act,
        ) = saved
        onehot, chosen = tables(expert_ids, slot_ids)
        d_norm_two = jnp.einsum("tjs,sd->td", onehot, d_back, preferred_element_type=jnp.float32)
        d_norm_two = d_norm_two + jnp.einsum(
            "te,de->td", d_logits, weight_router, preferred_element_type=jnp.float32
        )
        normed_two, unit_two, inverse_two = norm_forward(middle, gain_rows[1], shift_rows[1])
        d_middle_norm, gain_two, shift_two = norm_backward(
            d_norm_two, unit_two, inverse_two, gain_rows[1]
        )
        d_middle = d_out + d_middle_norm
        d_middle_half = d_middle.astype(jnp.bfloat16)
        d_attended = jnp.einsum(
            "te,de->td", d_middle_half, weight_out, preferred_element_type=jnp.float32
        ).astype(jnp.bfloat16)
        d_qkv = attend_backward(qkv_rows, log_totals, d_attended, local_images)
        d_norm_one = jnp.einsum("te,de->td", d_qkv, weight_qkv, preferred_element_type=jnp.float32)
        normed_one, unit_one, inverse_one = norm_forward(inputs, gain_rows[0], shift_rows[0])
        d_input_norm, gain_one, shift_one = norm_backward(
            d_norm_one, unit_one, inverse_one, gain_rows[0]
        )
        d_input = d_middle + d_input_norm
        return (
            d_input,
            d_middle_half,
            d_qkv,
            jnp.stack([gain_one, gain_two]),
            jnp.stack([shift_one, shift_two]),
        )

    received = jnp.zeros((token_rows, model_width), jnp.float32)
    kept_saved = []
    layer_outs = []
    for tick_index in range(MB + 1):
        micro_index = tick_index - section_index
        pick_index = jnp.clip(micro_index, 0, MB - 1)
        inputs = jnp.where(is_first, owned_rows[min(tick_index, MB - 1)], received)
        route_now = lax.dynamic_index_in_dim(route_rows, pick_index, 0, keepdims=False)
        slot_now = lax.dynamic_index_in_dim(slot_rows, pick_index, 0, keepdims=False)
        (
            forward_norm_one,
            forward_qkv_rows,
            forward_log_totals,
            forward_attended,
            forward_middle,
            forward_norm_two,
            forward_gate_pair,
            forward_outbound,
        ) = forward_front(inputs, route_now, slot_now)
        forward_inbound = lax.all_to_all(
            forward_outbound, "expert", split_axis=0, concat_axis=1, tiled=True
        )
        all_rows = lax.all_gather(forward_inbound, "dp", axis=1, tiled=True)
        expert_pre_act = jnp.einsum(
            "erd,edf->erf", all_rows, weight_up, preferred_element_type=jnp.float32
        )
        expert_hidden = jax.nn.gelu(expert_pre_act, approximate=False).astype(jnp.bfloat16)
        partial_out = jnp.einsum(
            "erf,efd->erd", expert_hidden, weight_down, preferred_element_type=jnp.float32
        )
        experts_pieces = lax.all_to_all(
            partial_out[None], "dp", split_axis=2, concat_axis=0, tiled=True
        )
        result = jnp.sum(experts_pieces, axis=0).astype(jnp.bfloat16)
        forward_back_rows = lax.all_to_all(
            result, "expert", split_axis=1, concat_axis=0, tiled=True
        ).reshape(expert_count * capacity, model_width)
        forward_onehot, forward_chosen = tables(route_now, slot_now)
        forward_selected = jnp.einsum(
            "tjs,sd->tjd", forward_onehot, forward_back_rows, preferred_element_type=jnp.float32
        )
        out_rows = forward_middle + jnp.sum(
            forward_gate_pair[:, :, None] * forward_selected, axis=1
        )
        forward_saved = (
            inputs,
            forward_norm_one,
            forward_qkv_rows,
            forward_log_totals,
            forward_attended,
            forward_middle,
            forward_norm_two,
            forward_gate_pair,
            forward_back_rows,
            forward_inbound,
            expert_pre_act,
        )
        out_rows, saved = (out_rows, forward_saved)
        kept_saved.append(saved)
        layer_outs.append(out_rows)
        if tick_index < MB:
            received = shifted(out_rows.astype(jnp.bfloat16), "section", 1).astype(jnp.float32)
    stacked = jax.tree.map(lambda *stack_parts: jnp.stack(stack_parts), *kept_saved)
    returned = jnp.zeros((token_rows, model_width), jnp.float32)
    grad_list = []
    records = []
    gain_total = None
    shift_total = None
    for tick_index in range(MB + 1):
        micro_index = tick_index - 1 + section_index
        active = (micro_index >= 0) & (micro_index < MB)
        pick_index = jnp.clip(micro_index, 0, MB - 1)
        saved_index = jnp.clip(tick_index - 1 + 2 * section_index, 0, MB)
        saved_now = jax.tree.map(
            lambda stack_part: lax.dynamic_index_in_dim(stack_part, saved_index, 0, keepdims=False),
            stacked,
        )
        cotangent = jnp.where(is_first, returned, owned_rows[min(tick_index, MB - 1)])
        cotangent = jnp.where(active, cotangent, jnp.zeros_like(cotangent))
        route_now = lax.dynamic_index_in_dim(route_rows, pick_index, 0, keepdims=False)
        slot_now = lax.dynamic_index_in_dim(slot_rows, pick_index, 0, keepdims=False)
        (
            backward_inputs,
            backward_norm_one,
            backward_qkv_rows,
            backward_log_totals,
            backward_attended,
            backward_middle,
            backward_norm_two,
            backward_gate_pair,
            backward_back_rows,
            backward_inbound,
            backward_pre_act,
        ) = saved_now
        backward_d_logits, backward_d_outbound = backward_front(
            cotangent, backward_gate_pair, backward_back_rows, route_now, slot_now
        )
        d_arrived = lax.all_to_all(
            backward_d_outbound, "expert", split_axis=0, concat_axis=1, tiled=True
        )
        experts_grads_in = lax.all_gather(d_arrived, "dp", axis=1, tiled=True)
        rows_in = lax.all_gather(backward_inbound, "dp", axis=1, tiled=True)
        hidden = jax.nn.gelu(backward_pre_act, approximate=False).astype(jnp.bfloat16)
        d_hidden = jnp.einsum(
            "erd,efd->erf", experts_grads_in, weight_down, preferred_element_type=jnp.float32
        )
        d_pre = (d_hidden * gelu_slope(backward_pre_act)).astype(jnp.bfloat16)
        partial_in = jnp.einsum(
            "erf,edf->erd", d_pre, weight_up, preferred_element_type=jnp.float32
        )
        pieces = lax.all_to_all(
            partial_in[None].astype(jnp.bfloat16), "dp", split_axis=2, concat_axis=0, tiled=True
        ).astype(jnp.float32)
        d_inbound = jnp.sum(pieces, axis=0).astype(jnp.bfloat16)
        expert_record = (rows_in, experts_grads_in, d_pre, hidden)
        backward_d_back = lax.all_to_all(
            d_inbound, "expert", split_axis=1, concat_axis=0, tiled=True
        ).reshape(expert_count * capacity, model_width)
        backward_d_input, backward_d_middle_half, backward_d_qkv, gain_part, shift_part = (
            backward_finish(
                cotangent, saved_now, backward_d_back, backward_d_logits, route_now, slot_now
            )
        )
        record = (
            backward_norm_one,
            backward_d_qkv,
            backward_attended,
            backward_d_middle_half,
            backward_norm_two,
            backward_d_logits,
            expert_record,
        )
        d_input, record, gain_part, shift_part = (backward_d_input, record, gain_part, shift_part)
        grad_list.append(d_input)
        records.append(record)
        gain_total = gain_part if gain_total is None else gain_total + gain_part
        shift_total = shift_part if shift_total is None else shift_total + shift_part
        if tick_index < MB:
            returned = shifted(d_input.astype(jnp.bfloat16), "section", -1).astype(jnp.float32)
    norm_one_all = jnp.stack([item[0] for item in records])
    d_qkv_all = jnp.stack([item[1] for item in records])
    attended_all = jnp.stack([item[2] for item in records])
    d_middle_all = jnp.stack([item[3] for item in records])
    norm_two_all = jnp.stack([item[4] for item in records])
    d_logits_all = jnp.stack([item[5] for item in records])
    rows_all = jnp.stack([item[6][0] for item in records])
    grads_all = jnp.stack([item[6][1] for item in records])
    d_pre_all = jnp.stack([item[6][2] for item in records])
    hidden_all = jnp.stack([item[6][3] for item in records])
    qkv_grad = jnp.einsum(
        "ktd,kte->de", norm_one_all, d_qkv_all, preferred_element_type=jnp.float32
    )
    out_grad = jnp.einsum(
        "ktd,kte->de", attended_all, d_middle_all, preferred_element_type=jnp.float32
    )
    router_grad = jnp.einsum(
        "ktd,kte->de", norm_two_all, d_logits_all, preferred_element_type=jnp.float32
    )
    up_grad = jnp.einsum("kerd,kerf->edf", rows_all, d_pre_all, preferred_element_type=jnp.float32)
    dense_shards = (
        lax.psum_scatter(qkv_grad[None], ("dp", "expert"), scatter_dimension=1, tiled=True),
        lax.psum_scatter(out_grad[None], ("dp", "expert"), scatter_dimension=1, tiled=True),
        lax.psum_scatter(router_grad[None], ("dp", "expert"), scatter_dimension=1, tiled=True),
        lax.psum_scatter(gain_total[None], ("dp", "expert"), scatter_dimension=2, tiled=True),
        lax.psum_scatter(shift_total[None], ("dp", "expert"), scatter_dimension=2, tiled=True),
    )
    down_grad = jnp.einsum(
        "kerf,kerd->efd", hidden_all, grads_all, preferred_element_type=jnp.float32
    )
    up_shard = up_grad[None]
    down_shard = down_grad[None]
    boundary_rows = jnp.where(is_first, jnp.stack(grad_list[1:]), jnp.stack(layer_outs[1:]))
    boundary_out = boundary_rows.reshape(1, MB, local_images, boundary_in.shape[3], model_width)
    return (
        boundary_out,
        dense_shards[3],
        dense_shards[4],
        dense_shards[0],
        dense_shards[1],
        dense_shards[2],
        up_shard,
        down_shard,
    )


def solution(mesh):
    in_specs = (
        P("section", None, ("dp", "expert"), None, None),
        P("section", None, ("dp", "expert"), None, None),
        P("section", None, ("dp", "expert"), None, None),
        P("section", None, ("dp", "expert")),
        P("section", None, ("dp", "expert")),
        P("section", ("dp", "expert"), None),
        P("section", ("dp", "expert"), None),
        P("section", ("dp", "expert"), None),
        P("section", "expert", None, "dp"),
        P("section", "expert", "dp", None),
    )
    out_specs = (
        P("section", None, ("dp", "expert"), None, None),
        P("section", None, ("dp", "expert")),
        P("section", None, ("dp", "expert")),
        P("section", ("dp", "expert"), None),
        P("section", ("dp", "expert"), None),
        P("section", ("dp", "expert"), None),
        P("section", "expert", None, "dp"),
        P("section", "expert", "dp", None),
    )
    return jax.shard_map(
        on_device, mesh=mesh, in_specs=in_specs, out_specs=out_specs, check_vma=False
    )
```

profile of v0, /device:TPU:0, one launch (start us, length us, event | category | flops | bytes accessed | tf_op | source)
XLA Modules:
  0.0 1960.0 jit_solution(10724974196611161775)
XLA Ops:
  9.5 45.1 %all_gather.43 = bf16[1,2,768]{1,0,2:T(2,128)(2,1)S(1)} all-gather(bf16[1,2,48]{1,0,2:T(2,128)(2,1)S(1)} %copy.412), channel_id=1, replica_groups=mesh['section'=2,'dp'=4,'expert'=4] {'dp','expert'}, dimensions={2}, use_global_device_ids=true | all-gather | bytes 3264 | tf_op jit(solution)/shard_map/all_gather | solution.py:127
  55.8 39.5 %all_gather.42 = bf16[1,2,768]{1,0,2:T(2,128)(2,1)S(1)} all-gather(bf16[1,2,48]{1,0,2:T(2,128)(2,1)S(1)} %copy.411), channel_id=1, replica_groups=mesh['section'=2,'dp'=4,'expert'=4] {'dp','expert'}, dimensions={2}, use_global_device_ids=true | all-gather | bytes 3264 | tf_op jit(solution)/shard_map/all_gather | solution.py:126
  127.4 19.6 %all-gather.17.cloned.1.call-done = bf16[1,768,768]{2,1,0:T(8,128)(2,1)} async-done(((bf16[1,48,768]{2,1,0:T(8,128)(2,1)}), bf16[1,768,768]{2,1,0:T(8,128)(2,1)}) %all-gather.17.cloned.1.call-update) | async-done | bytes 1179664 | tf_op jit(solution)/shard_map/all_gather | solution.py:124
  161.9 41.7 %all-gather.19.cloned.1.call-done = bf16[2,640,768]{2,1,0:T(8,128)(2,1)} async-done(((bf16[2,160,768]{2,1,0:T(8,128)(2,1)}), bf16[2,640,768]{2,1,0:T(8,128)(2,1)}) %all-gather.19.cloned.1.call-update) | async-done | bytes 1966096 | tf_op jit(solution)/shard_map/all_gather | solution.py:244
  229.7 114.1 %all_gather.46 = bf16[1,768,8]{2,0,1:T(2,128)(2,1)} all-gather(bf16[1,48,8]{2,0,1:T(2,128)(2,1)S(1)} %copy.418), channel_id=1, replica_groups=mesh['section'=2,'dp'=4,'expert'=4] {'dp','expert'}, dimensions={1}, use_global_device_ids=true | all-gather | bytes 13056 | tf_op jit(solution)/shard_map/all_gather | solution.py:125
  379.0 11.5 all_to_all.271
  391.3 43.8 %all-gather.21.cloned.1.call-done = bf16[2,640,768]{2,1,0:T(8,128)(2,1)} async-done(((bf16[2,160,768]{2,1,0:T(8,128)(2,1)}), bf16[2,640,768]{2,1,0:T(8,128)(2,1)}) %all-gather.21.cloned.1.call-update) | async-done | bytes 1966096 | tf_op jit(solution)/shard_map/all_gather | solution.py:244
  461.4 87.5 %all-to-all-done.4 = f32[1,2,640,768]{3,1,0,2:T(2,128)} async-done(((f32[1,2,640,768]{3,1,0,2:T(2,128)}), f32[1,2,640,768]{3,1,0,2:T(2,128)}, u32[]{:S(2)}, u32[]{:S(2)}) %all-to-all-start.4) | async-done | bytes 3932192 | tf_op jit(solution)/shard_map/all_to_all | solution.py:252
  584.3 11.5 all_to_all.272
  611.7 25.7 %all-gather.25.cloned.1.call-done = bf16[2,640,768]{2,1,0:T(8,128)(2,1)} async-done(((bf16[2,160,768]{2,1,0:T(8,128)(2,1)}), bf16[2,640,768]{2,1,0:T(8,128)(2,1)}) %all-gather.25.cloned.1.call-update) | async-done | bytes 1966096 | tf_op jit(solution)/shard_map/all_gather | solution.py:244
  649.3 31.9 %all-gather.23.cloned.1.call-done = bf16[2,640,768]{2,1,0:T(8,128)(2,1)} async-done(((bf16[2,160,768]{2,1,0:T(8,128)(2,1)}), bf16[2,640,768]{2,1,0:T(8,128)(2,1)}) %all-gather.23.cloned.1.call-update) | async-done | bytes 1966096 | tf_op jit(solution)/shard_map/all_gather | solution.py:322
  696.8 12.3 fusion.180
  714.1 28.2 %all-to-all-done.8 = bf16[1,2,640,768]{3,1,0,2:T(2,128)(2,1)} async-done(((bf16[1,2,640,768]{3,1,0,2:T(2,128)(2,1)}), bf16[1,2,640,768]{3,1,0,2:T(2,128)(2,1)}, u32[]{:S(2)}, u32[]{:S(2)}) %all-to-all-start.8) | async-done | bytes 1966112 | tf_op jit(solution)/shard_map/all_to_all | solution.py:332
  767.9 66.6 %all-to-all-done.10 = f32[1,2,640,768]{3,1,0,2:T(2,128)} async-done(((f32[1,2,640,768]{3,1,0,2:T(2,128)}), f32[1,2,640,768]{3,1,0,2:T(2,128)}, u32[]{:S(2)}, u32[]{:S(2)}) %all-to-all-start.10) | async-done | bytes 3932192 | tf_op jit(solution)/shard_map/all_to_all | solution.py:252
  909.1 40.4 %all-gather.27.cloned.1.call-done = bf16[2,640,768]{2,1,0:T(8,128)(2,1)} async-done(((bf16[2,160,768]{2,1,0:T(8,128)(2,1)}), bf16[2,640,768]{2,1,0:T(8,128)(2,1)}) %all-gather.27.cloned.1.call-update) | async-done | bytes 1966096 | tf_op jit(solution)/shard_map/all_gather | solution.py:322
  977.6 32.7 %all-to-all-done.13 = bf16[1,2,640,768]{3,1,0,2:T(2,128)(2,1)} async-done(((bf16[1,2,640,768]{3,1,0,2:T(2,128)(2,1)}), bf16[1,2,640,768]{3,1,0,2:T(2,128)(2,1)}, u32[]{:S(2)}, u32[]{:S(2)}) %all-to-all-start.13) | async-done | bytes 1966112 | tf_op jit(solution)/shard_map/all_to_all | solution.py:332
  1083.2 35.8 %all-gather.29.cloned.1.call-done = bf16[2,640,768]{2,1,0:T(8,128)(2,1)} async-done(((bf16[2,160,768]{2,1,0:T(8,128)(2,1)}), bf16[2,640,768]{2,1,0:T(8,128)(2,1)}) %all-gather.29.cloned.1.call-update) | async-done | bytes 1966096 | tf_op jit(solution)/shard_map/all_gather | solution.py:322
  1165.5 39.3 %all-to-all-done.16 = bf16[1,2,640,768]{3,1,0,2:T(2,128)(2,1)} async-done(((bf16[1,2,640,768]{3,1,0,2:T(2,128)(2,1)}), bf16[1,2,640,768]{3,1,0,2:T(2,128)(2,1)}, u32[]{:S(2)}, u32[]{:S(2)}) %all-to-all-start.16) | async-done | bytes 1966112 | tf_op jit(solution)/shard_map/all_to_all | solution.py:332
  1300.9 27.8 %fusion.50 = (bf16[1,2,640,768]{3,2,1,0:T(8,128)(2,1)}, bf16[1,2,640,768]{3,2,1,0:T(8,128)(2,1)}, bf16[1,2,640,768]{3,2,1,0:T(8,128)(2,1)}) fusion(f32[3,2,640,768]{3,2,1,0:T(8,128)} %pad_maximum_fusion, s32[]{:T(128)S(6)} %min.30, s32[]{:T(128)S(6)} %min.33, s32[]{:T(128)S(6)} %min.35), kind=kLoop, calls=%fused_computation.62 | loop fusion | flops 191692800 | bytes 17694732 | tf_op jit(solution)/shard_map/convert_element_type | solution.py:324
  1329.4 80.7 %reduce-scatter.20.cloned.1.call-done = f32[48,8]{1,0:T(8,128)} async-done(((f32[768,8]{1,0:T(8,128)}), f32[48,8]{1,0:T(8,128)}) %reduce-scatter.20.cloned.1.call-update) | async-done | bytes 1552
  1433.4 103.5 %reduce-scatter.16.cloned.1.call-done = f32[48,2]{1,0:T(8,128)} async-done(((f32[768,2]{1,0:T(8,128)}), f32[48,2]{1,0:T(8,128)}) %reduce-scatter.16.cloned.1.call-update) | async-done | bytes 400
  1538.3 125.3 %reduce-scatter.18.cloned.1.call-done = f32[48,2]{1,0:T(8,128)} async-done(((f32[768,2]{1,0:T(8,128)}), f32[48,2]{1,0:T(8,128)}) %reduce-scatter.18.cloned.1.call-update) | async-done | bytes 400
  1665.0 131.8 %reduce-scatter.14.cloned.1.call-done = f32[1,48,768]{2,1,0:T(8,128)} async-done(((f32[1,768,768]{2,1,0:T(8,128)}), f32[1,48,768]{2,1,0:T(8,128)}) %reduce-scatter.14.cloned.1.call-update) | async-done | bytes 147472 | tf_op jit(solution)/shard_map/reduce_scatter | solution.py:383
  1796.8 156.5 %reduce-scatter.12.cloned.1.call-done = f32[1,48,2304]{2,1,0:T(8,128)} async-done(((f32[1,768,2304]{2,1,0:T(8,128)}), f32[1,48,2304]{2,1,0:T(8,128)}) %reduce-scatter.12.cloned.1.call-update) | async-done | bytes 442384 | tf_op jit(solution)/shard_map/reduce_scatter | solution.py:382
  (711 shorter events, 590.4 us)
Async XLA Ops:
  7.2 107.2 %all-gather.15.cloned.1.call-start = ((), (), s32[]{:S(2)}) async-start(), calls=%async_computation.23 | async-start | bytes 3760128 | tf_op jit(solution)/shard_map/all_gather | solution.py:123
  7.9 139.1 %all-gather.17.cloned.1.call-start = ((), (), s32[]{:S(2)}) async-start(), calls=%async_computation.24 | async-start | bytes 1253376 | tf_op jit(solution)/shard_map/all_gather | solution.py:124
  8.7 194.9 %all-gather.19.cloned.1.call-start = ((), (), s32[]{:S(2)}) async-start(), calls=%async_computation.25 | async-start | bytes 2457600 | tf_op jit(solution)/shard_map/all_gather | solution.py:244
  224.7 120.5 %all-to-all-start.1 = ((f32[1,2,640,768]{3,1,0,2:T(2,128)}), f32[1,2,640,768]{3,1,0,2:T(2,128)}, u32[]{:S(2)}, u32[]{:S(2)}) async-start(f32[1,2,640,768]{3,1,0,2:T(2,128)} %copy.421), calls=%async_computation.1 | async-start | bytes 7864320 | tf_op jit(solution)/shard_map/all_to_all | solution.py:252
  353.6 81.5 %all-gather.21.cloned.1.call-start = ((), (), s32[]{:S(2)}) async-start(), calls=%async_computation.26 | async-start | bytes 2457600 | tf_op jit(solution)/shard_map/all_gather | solution.py:244
  456.5 92.4 %all-to-all-start.4 = ((f32[1,2,640,768]{3,1,0,2:T(2,128)}), f32[1,2,640,768]{3,1,0,2:T(2,128)}, u32[]{:S(2)}, u32[]{:S(2)}) async-start(f32[1,2,640,768]{3,1,0,2:T(2,128)} %copy.429), calls=%async_computation.4 | async-start | bytes 7864320 | tf_op jit(solution)/shard_map/all_to_all | solution.py:252
  557.4 80.0 %all-gather.25.cloned.1.call-start = ((), (), s32[]{:S(2)}) async-start(), calls=%async_computation.28 | async-start | bytes 2457600 | tf_op jit(solution)/shard_map/all_gather | solution.py:244
  596.6 84.6 %all-gather.23.cloned.1.call-start = ((), (), s32[]{:S(2)}) async-start(), calls=%async_computation.27 | async-start | bytes 2457600 | tf_op jit(solution)/shard_map/all_gather | solution.py:322
  692.1 50.2 %all-to-all-start.8 = ((bf16[1,2,640,768]{3,1,0,2:T(2,128)(2,1)}), bf16[1,2,640,768]{3,1,0,2:T(2,128)(2,1)}, u32[]{:S(2)}, u32[]{:S(2)}) async-start(bf16[1,2,640,768]{3,1,0,2:T(2,128)(2,1)} %copy.438), calls=%async_computation.8 | async-start | bytes 3932160 | tf_op jit(solution)/shard_map/all_to_all | solution.py:332
  742.3 92.2 %all-to-all-start.10 = ((f32[1,2,640,768]{3,1,0,2:T(2,128)}), f32[1,2,640,768]{3,1,0,2:T(2,128)}, u32[]{:S(2)}, u32[]{:S(2)}) async-start(f32[1,2,640,768]{3,1,0,2:T(2,128)} %copy.443), calls=%async_computation.10 | async-start | bytes 7864320 | tf_op jit(solution)/shard_map/all_to_all | solution.py:252
  834.5 12.0 all-to-all-start.9
  850.8 98.6 %all-gather.27.cloned.1.call-start = ((), (), s32[]{:S(2)}) async-start(), calls=%async_computation.29 | async-start | bytes 2457600 | tf_op jit(solution)/shard_map/all_gather | solution.py:322
  960.4 49.9 %all-to-all-start.13 = ((bf16[1,2,640,768]{3,1,0,2:T(2,128)(2,1)}), bf16[1,2,640,768]{3,1,0,2:T(2,128)(2,1)}, u32[]{:S(2)}, u32[]{:S(2)}) async-start(bf16[1,2,640,768]{3,1,0,2:T(2,128)(2,1)} %copy.454), calls=%async_computation.13 | async-start | bytes 3932160 | tf_op jit(solution)/shard_map/all_to_all | solution.py:332
  1018.6 100.3 %all-gather.29.cloned.1.call-start = ((), (), s32[]{:S(2)}) async-start(), calls=%async_computation.30 | async-start | bytes 2457600 | tf_op jit(solution)/shard_map/all_gather | solution.py:322
  1078.1 202.5 %all-gather.35.cloned.1.call-start = ((), (), s32[]{:S(2)}) async-start(), calls=%async_computation.35 | async-start | bytes 2457600 | tf_op jit(solution)/shard_map/all_gather | solution.py:323
  1081.6 205.9 %all-gather.33.cloned.1.call-start = ((), (), s32[]{:S(2)}) async-start(), calls=%async_computation.34 | async-start | bytes 2457600 | tf_op jit(solution)/shard_map/all_gather | solution.py:323
  1129.9 74.9 %all-to-all-start.16 = ((bf16[1,2,640,768]{3,1,0,2:T(2,128)(2,1)}), bf16[1,2,640,768]{3,1,0,2:T(2,128)(2,1)}, u32[]{:S(2)}, u32[]{:S(2)}) async-start(bf16[1,2,640,768]{3,1,0,2:T(2,128)(2,1)} %copy.465), calls=%async_computation.16 | async-start | bytes 3932160 | tf_op jit(solution)/shard_map/all_to_all | solution.py:332
  1134.5 159.6 %all-gather.31.cloned.1.call-start = ((), (), s32[]{:S(2)}) async-start(), calls=%async_computation.33 | async-start | bytes 2457600 | tf_op jit(solution)/shard_map/all_gather | solution.py:323
  1209.5 12.3 all-to-all-start.17
  1213.6 196.5 %reduce-scatter.20.cloned.1.call-start = ((), (), s32[]{:S(2)}) async-start(), calls=%async_computation.38 | async-start | bytes 417792
  1215.1 321.8 %reduce-scatter.16.cloned.1.call-start = ((), (), s32[]{:S(2)}) async-start(), calls=%async_computation.36 | async-start | bytes 417792
  1254.5 409.1 %reduce-scatter.18.cloned.1.call-start = ((), (), s32[]{:S(2)}) async-start(), calls=%async_computation.37 | async-start | bytes 417792
  1255.6 541.2 %reduce-scatter.14.cloned.1.call-start = ((), (), s32[]{:S(2)}) async-start(), calls=%async_computation.32 | async-start | bytes 2506752 | tf_op jit(solution)/shard_map/reduce_scatter | solution.py:383
  1259.8 693.4 %reduce-scatter.12.cloned.1.call-start = ((), (), s32[]{:S(2)}) async-start(), calls=%async_computation.31 | async-start | bytes 7520256 | tf_op jit(solution)/shard_map/reduce_scatter | solution.py:382
  (187 other events, 3692.6 us)
Sparse Core Ops, SparseCore 0:
  10.8 78.3 all-gather.14
  92.0 55.0 all-gather.16
  162.0 41.5 all-gather.18
  391.5 43.5 all-gather.20
  596.7 40.6 all-gather.24
  638.8 42.3 all-gather.22
  909.2 40.1 all-gather.26
  1078.2 40.6 all-gather.28
  1120.5 75.7 all-gather.34
  1197.8 41.9 all-gather.32
  1241.3 42.3 all-gather.30
  1288.2 121.8 reduce-scatter.19
  1414.8 122.0 reduce-scatter.15
  1541.4 122.1 reduce-scatter.17
  1668.9 127.8 reduce-scatter.13
  1802.5 150.6 reduce-scatter.11
where the time goes:
time: 1970 us; the launch traced here: 1960 us
  waiting for transfers between devices  1130 us (57%)
  blocking collectives  264 us (13%)
  matrix products  218 us (11%)
  local copies, waits for them, and re-layouts  167 us (8%)
  other arithmetic  107 us (5%)
  starting transfers between devices  59.6 us (3%)
    unnamed x19, waiting for transfers between devices  311 us
    reduce_scatter x1, waiting for transfers between devices, on_device(): lax.psum_scatter(qkv_grad[None], ('dp', 'expert'), scatter_dimension=1, t...  156 us
    all_to_all x3, waiting for transfers between devices, on_device(): lax.all_to_all(partial_out[None], 'dp', split_axis=2, concat_axis=0, tile...  154 us
    reduce_scatter x1, waiting for transfers between devices, on_device(): lax.psum_scatter(out_grad[None], ('dp', 'expert'), scatter_dimension=1, t...  132 us
    all_gather x1, blocking collectives, on_device(): lax.all_gather(w_router, ('dp', 'expert'), axis=1, tiled=True)  114 us
    all_gather x3, waiting for transfers between devices, on_device(): all_rows = lax.all_gather(forward_inbound, 'dp', axis=1, tiled=True)  111 us
    all_gather x3, waiting for transfers between devices, on_device(): experts_grads_in = lax.all_gather(d_arrived, 'dp', axis=1, tiled=True)  108 us
    all_to_all x3, waiting for transfers between devices, on_device(): lax.all_to_all(partial_in[None].astype(jnp.bfloat16), 'dp', split_axis=2,...  100 us
  transfers between devices with their start and end apart: 32, of which 26 were waited for; matrix products, arithmetic and copies ran while one was open for 15% of the time, Pallas kernels for 0%

commit v1 on v0

v1 whole, which is shorter than its diff:
```python
import math

import jax
import jax.numpy as jnp
from jax import lax
from jax.sharding import PartitionSpec as P

HEADS = 12
HEAD_DIM = 64
EXP_DEV = 2
MB = 2


EPS = 1e-06
SQRT_HALF = 0.7071067811865476
INV_ROOT_TAU = 0.3989422804014327


def norm_forward(values, gain_row, shift_row):
    centred = values - jnp.mean(values, axis=-1, keepdims=True)
    variance = jnp.mean(centred * centred, axis=-1, keepdims=True)
    inverse = lax.rsqrt(variance + EPS)
    unit_rows = centred * inverse
    return (unit_rows * gain_row + shift_row, unit_rows, inverse)


def norm_backward(d_normed, unit_rows, inverse, gain_row):
    d_gain = jnp.sum(d_normed * unit_rows, axis=0)
    d_shift = jnp.sum(d_normed, axis=0)
    scaled = d_normed * gain_row
    d_values = inverse * (
        scaled
        - jnp.mean(scaled, axis=-1, keepdims=True)
        - unit_rows * jnp.mean(scaled * unit_rows, axis=-1, keepdims=True)
    )
    return (d_values, d_gain, d_shift)


def gelu_slope(pre_act):
    return (
        0.5 * (1.0 + lax.erf(pre_act * SQRT_HALF))
        + pre_act * jnp.exp(-0.5 * pre_act * pre_act) * INV_ROOT_TAU
    )


def split_heads(qkv_rows, image_count):
    feature_count = qkv_rows.shape[1] // 3
    return [
        qkv_rows[:, part_index * feature_count : (part_index + 1) * feature_count].reshape(
            image_count, -1, HEADS, HEAD_DIM
        )
        for part_index in range(3)
    ]


def attend_forward(qkv_rows, image_count):
    queries, key_rows, value_rows = split_heads(qkv_rows, image_count)
    scale_factor = 1.0 / math.sqrt(HEAD_DIM)
    scores = (
        jnp.einsum("bqhd,bkhd->bhqk", queries, key_rows, preferred_element_type=jnp.float32)
        * scale_factor
    )
    log_totals = jnp.log(jnp.sum(jnp.exp(scores), axis=-1))
    probs_half = jnp.exp(scores - log_totals[..., None]).astype(jnp.bfloat16)
    attended = jnp.einsum(
        "bhqk,bkhd->bqhd", probs_half, value_rows, preferred_element_type=jnp.float32
    )
    return (attended.astype(jnp.bfloat16).reshape(-1, HEADS * HEAD_DIM), log_totals)


def attend_backward(qkv_rows, log_totals, d_attended, image_count):
    queries, key_rows, value_rows = split_heads(qkv_rows, image_count)
    scale_factor = 1.0 / math.sqrt(HEAD_DIM)
    scores = (
        jnp.einsum("bqhd,bkhd->bhqk", queries, key_rows, preferred_element_type=jnp.float32)
        * scale_factor
    )
    probs = jnp.exp(scores - log_totals[..., None])
    probs_half = probs.astype(jnp.bfloat16)
    d_heads = d_attended.reshape(image_count, -1, HEADS, HEAD_DIM)
    d_values = jnp.einsum(
        "bhqk,bqhd->bkhd", probs_half, d_heads, preferred_element_type=jnp.float32
    )
    d_probs = jnp.einsum("bqhd,bkhd->bhqk", d_heads, value_rows, preferred_element_type=jnp.float32)
    row_dot = jnp.sum(probs * d_probs, axis=-1, keepdims=True)
    d_scores = (probs * (d_probs - row_dot) * scale_factor).astype(jnp.bfloat16)
    d_queries = jnp.einsum(
        "bhqk,bkhd->bqhd", d_scores, key_rows, preferred_element_type=jnp.float32
    )
    d_keys = jnp.einsum("bhqk,bqhd->bkhd", d_scores, queries, preferred_element_type=jnp.float32)
    feature_count = HEADS * HEAD_DIM
    joined = jnp.concatenate(
        [
            d_queries.reshape(-1, feature_count),
            d_keys.reshape(-1, feature_count),
            d_values.reshape(-1, feature_count),
        ],
        axis=1,
    )
    return joined.astype(jnp.bfloat16)


def on_device(
    boundary_in, routes, capacity_slots, ln_gain, ln_bias, w_qkv, w_out, w_router, w_up, w_down
):
    section_index = lax.axis_index("section")
    is_first = section_index == 0
    expert_count = EXP_DEV * lax.axis_size("expert")
    local_images = boundary_in.shape[2]
    token_rows = local_images * boundary_in.shape[3]
    model_width = boundary_in.shape[4]
    capacity = 26 * token_rows // (16 * expert_count)
    chips = ("dp", "expert")
    half = jnp.bfloat16

    def by_micro(values):
        return lax.all_to_all(values, "section", split_axis=0, concat_axis=0, tiled=True)

    edge_rows = by_micro(boundary_in[0].reshape(MB, token_rows, model_width))
    route_rows = by_micro(routes[0].reshape(MB, token_rows, 2))
    slot_rows = by_micro(capacity_slots[0].reshape(MB, token_rows, 2))

    def both_layers(shard, axis):
        whole = lax.all_gather(shard, chips, axis=axis, tiled=True)
        return lax.all_gather(whole, "section", axis=0, tiled=True)

    gain_all = both_layers(ln_gain, 2).astype(jnp.float32)
    shift_all = both_layers(ln_bias, 2).astype(jnp.float32)
    qkv_all = both_layers(w_qkv, 1)
    out_all = both_layers(w_out, 1)
    router_all = both_layers(w_router, 1)
    up_all = lax.all_gather(w_up, "section", axis=0, tiled=True)
    down_all = lax.all_gather(w_down, "section", axis=0, tiled=True)

    def tables(expert_ids, slot_ids):
        slot_index = jnp.where(slot_ids < capacity, expert_ids * capacity + slot_ids, -1)
        columns = jnp.arange(expert_count * capacity, dtype=jnp.int32)
        onehot = (slot_index[:, :, None] == columns).astype(half)
        chosen = (expert_ids[:, :, None] == jnp.arange(expert_count, dtype=jnp.int32)).astype(
            jnp.float32
        )
        return (onehot, chosen)

    def to_experts(rows):
        blocks = rows.reshape(expert_count, capacity, model_width)
        arrived = lax.all_to_all(blocks, "expert", split_axis=0, concat_axis=1, tiled=True)
        return lax.all_gather(arrived, "dp", axis=1, tiled=True)

    def from_experts(partial):
        pieces = lax.all_to_all(
            partial.astype(half)[None], "dp", split_axis=2, concat_axis=0, tiled=True
        )
        total = jnp.sum(pieces.astype(jnp.float32), axis=0).astype(half)
        return lax.all_to_all(
            total, "expert", split_axis=1, concat_axis=0, tiled=True
        ).reshape(expert_count * capacity, model_width)

    def layer_forward(layer, inputs):
        onehot, chosen = tables(route_rows[layer], slot_rows[layer])
        normed_one, unit_one, inverse_one = norm_forward(
            inputs, gain_all[layer, 0], shift_all[layer, 0]
        )
        norm_one = normed_one.astype(half)
        qkv_rows = jnp.dot(norm_one, qkv_all[layer], preferred_element_type=jnp.float32).astype(half)
        attended, log_totals = attend_forward(qkv_rows, local_images)
        middle = inputs + jnp.dot(attended, out_all[layer], preferred_element_type=jnp.float32)
        normed_two, unit_two, inverse_two = norm_forward(
            middle, gain_all[layer, 1], shift_all[layer, 1]
        )
        norm_two = normed_two.astype(half)
        logits = jnp.dot(norm_two, router_all[layer], preferred_element_type=jnp.float32)
        picked = jnp.sum(logits[:, None, :] * chosen, axis=-1)
        leading = jax.nn.sigmoid(picked[:, 0] - picked[:, 1])
        gate_pair = jnp.stack([leading, 1.0 - leading], axis=-1)
        buffer = jnp.einsum(
            "tjs,td->sd", onehot, norm_two, preferred_element_type=jnp.float32
        ).astype(half)
        all_rows = to_experts(buffer)
        pre_act = jnp.einsum(
            "erd,edf->erf", all_rows, up_all[layer], preferred_element_type=jnp.float32
        )
        hidden = jax.nn.gelu(pre_act, approximate=False).astype(half)
        partial_out = jnp.einsum(
            "erf,efd->erd", hidden, down_all[layer], preferred_element_type=jnp.float32
        )
        back_rows = from_experts(partial_out)
        selected = jnp.einsum(
            "tjs,sd->tjd", onehot, back_rows, preferred_element_type=jnp.float32
        )
        out_rows = middle + jnp.sum(gate_pair[:, :, None] * selected, axis=1)
        saved = (
            inputs, norm_one, qkv_rows, log_totals, attended, middle, norm_two, gate_pair,
            back_rows, all_rows, pre_act, hidden,
        )
        return (out_rows, saved)

    def layer_backward(layer, d_out, saved):
        (
            inputs, norm_one, qkv_rows, log_totals, attended, middle, norm_two, gate_pair,
            back_rows, all_rows, pre_act, hidden,
        ) = saved
        onehot, chosen = tables(route_rows[layer], slot_rows[layer])
        weighted = (gate_pair[:, :, None] * d_out[:, None, :]).astype(half)
        d_buffer = jnp.einsum(
            "tjs,tjd->sd", onehot, weighted, preferred_element_type=jnp.float32
        ).astype(half)
        grads_in = to_experts(d_buffer)
        selected = jnp.einsum("tjs,sd->tjd", onehot, back_rows, preferred_element_type=jnp.float32)
        d_gate = jnp.sum(d_out[:, None, :] * selected, axis=-1)
        d_lead = (d_gate[:, 0] - d_gate[:, 1]) * gate_pair[:, 0] * gate_pair[:, 1]
        d_logits = (d_lead[:, None] * (chosen[:, 0] - chosen[:, 1])).astype(half)
        d_hidden = jnp.einsum(
            "erd,efd->erf", grads_in, down_all[layer], preferred_element_type=jnp.float32
        )
        d_pre = (d_hidden * gelu_slope(pre_act)).astype(half)
        partial_in = jnp.einsum(
            "erf,edf->erd", d_pre, up_all[layer], preferred_element_type=jnp.float32
        )
        d_back = from_experts(partial_in)
        up_grad = jnp.einsum("erd,erf->edf", all_rows, d_pre, preferred_element_type=jnp.float32)
        down_grad = jnp.einsum(
            "erf,erd->efd", hidden, grads_in, preferred_element_type=jnp.float32
        )
        owner_pairs = [(1 - layer, layer)]
        up_sent = lax.ppermute(up_grad.astype(half), "section", owner_pairs)
        down_sent = lax.ppermute(down_grad.astype(half), "section", owner_pairs)
        d_norm_two = jnp.einsum("tjs,sd->td", onehot, d_back, preferred_element_type=jnp.float32)
        d_norm_two = d_norm_two + jnp.einsum(
            "te,de->td", d_logits, router_all[layer], preferred_element_type=jnp.float32
        )
        normed_two, unit_two, inverse_two = norm_forward(
            middle, gain_all[layer, 1], shift_all[layer, 1]
        )
        d_middle_norm, gain_two, shift_two = norm_backward(
            d_norm_two, unit_two, inverse_two, gain_all[layer, 1]
        )
        d_middle = d_out + d_middle_norm
        d_middle_half = d_middle.astype(half)
        d_attended = jnp.einsum(
            "te,de->td", d_middle_half, out_all[layer], preferred_element_type=jnp.float32
        ).astype(half)
        d_qkv = attend_backward(qkv_rows, log_totals, d_attended, local_images)
        d_norm_one = jnp.einsum(
            "te,de->td", d_qkv, qkv_all[layer], preferred_element_type=jnp.float32
        )
        normed_one, unit_one, inverse_one = norm_forward(
            inputs, gain_all[layer, 0], shift_all[layer, 0]
        )
        d_input_norm, gain_one, shift_one = norm_backward(
            d_norm_one, unit_one, inverse_one, gain_all[layer, 0]
        )
        d_input = d_middle + d_input_norm
        operands = [
            lax.ppermute(item, "section", owner_pairs)
            for item in (norm_one, d_qkv, attended, d_middle_half)
        ]
        own = (norm_one, d_qkv, attended, d_middle_half)
        small = jnp.concatenate(
            [
                jnp.stack([gain_one, gain_two, shift_one, shift_two]),
                jnp.einsum("td,te->ed", norm_two, d_logits, preferred_element_type=jnp.float32),
            ]
        )
        return (d_input, own, operands, small, (up_grad, up_sent), (down_grad, down_sent))

    stream = edge_rows[0]
    saved_list = []
    for layer in range(2):
        if layer > 0:
            stream = stream.astype(half).astype(jnp.float32)
        stream, saved = layer_forward(layer, stream)
        saved_list.append(saved)
    cotangent = edge_rows[1]
    parts = [None, None]
    for layer in (1, 0):
        if layer < 1:
            cotangent = cotangent.astype(half).astype(jnp.float32)
        cotangent, *parts[layer] = layer_backward(layer, cotangent, saved_list[layer])

    def mine(first, second):
        return jnp.where(is_first, first, second)

    own = [mine(a, b) for a, b in zip(parts[0][0], parts[1][0])]
    other = [mine(a, b) for a, b in zip(parts[0][1], parts[1][1])]
    pairs = [jnp.stack([a, b]) for a, b in zip(own, other)]
    qkv_grad = jnp.einsum("ktd,kte->de", pairs[0], pairs[1], preferred_element_type=jnp.float32)
    out_grad = jnp.einsum("ktd,kte->de", pairs[2], pairs[3], preferred_element_type=jnp.float32)
    small_both = lax.psum(jnp.stack([parts[0][2], parts[1][2]]), "section")
    small_mine = mine(small_both[0], small_both[1])
    small_shard = lax.psum_scatter(small_mine, chips, scatter_dimension=1, tiled=True)
    qkv_shard = lax.psum_scatter(qkv_grad, chips, scatter_dimension=0, tiled=True)
    out_shard = lax.psum_scatter(out_grad, chips, scatter_dimension=0, tiled=True)

    def expert_grad(index):
        first = parts[0][index][0] + parts[0][index][1].astype(jnp.float32)
        second = parts[1][index][0] + parts[1][index][1].astype(jnp.float32)
        return mine(first, second)[None]

    up_shard = expert_grad(3)
    down_shard = expert_grad(4)
    boundary_rows = by_micro(jnp.stack([cotangent, stream]))
    boundary_out = boundary_rows.reshape(1, MB, local_images, boundary_in.shape[3], model_width)
    return (
        boundary_out,
        small_shard[None, 0:2],
        small_shard[None, 2:4],
        qkv_shard[None],
        out_shard[None],
        small_shard[4:].T[None],
        up_shard,
        down_shard,
    )


def solution(mesh):
    in_specs = (
        P("section", None, ("dp", "expert"), None, None),
        P("section", None, ("dp", "expert"), None, None),
        P("section", None, ("dp", "expert"), None, None),
        P("section", None, ("dp", "expert")),
        P("section", None, ("dp", "expert")),
        P("section", ("dp", "expert"), None),
        P("section", ("dp", "expert"), None),
        P("section", ("dp", "expert"), None),
        P("section", "expert", None, "dp"),
        P("section", "expert", "dp", None),
    )
    out_specs = (
        P("section", None, ("dp", "expert"), None, None),
        P("section", None, ("dp", "expert")),
        P("section", None, ("dp", "expert")),
        P("section", ("dp", "expert"), None),
        P("section", ("dp", "expert"), None),
        P("section", ("dp", "expert"), None),
        P("section", "expert", None, "dp"),
        P("section", "expert", "dp", None),
    )
    return jax.shard_map(
        on_device, mesh=mesh, in_specs=in_specs, out_specs=out_specs, check_vma=False
    )
```

time: 1970 us -> 1330 us (0.68)
  waiting for transfers between devices: 1130 us -> 734 us
  local copies, waits for them, and re-layouts: 167 us -> 64.5 us
  matrix products: 218 us -> 148 us
  blocking collectives: 264 us -> 207 us
  other arithmetic: 107 us -> 73.7 us
    unnamed x19 -> x15, waiting for transfers between devices: 311 us -> 43.6 us
    all_to_all x12 -> x10, waiting for transfers between devices: 282 us -> 110 us  [the longest x4 93.2 us: from_experts(): lax.all_to_all(partial.astype(half)[None], 'dp', split_axis=2, concat_axi...]
    dot_general x53 -> x36, matrix products: 157 us -> 91.4 us  [the longest x2 12.6 us: layer_forward(): jnp.einsum('erd,edf->erf', all_rows, up_all[layer], preferred_element_typ...]
    all_gather x3 -> x6, blocking collectives: 199 us -> 154 us  [the longest x3 148 us: both_layers(): whole = lax.all_gather(shard, chips, axis=axis, tiled=True)]
    all_gather x11 -> x10, waiting for transfers between devices: 239 us -> 278 us  [the longest x4 145 us: to_experts(): return lax.all_gather(arrived, 'dp', axis=1, tiled=True)]
    slice x23 -> x8, local copies, waits for them, and re-layouts: 36.8 us -> 5.15 us  [split_heads(): qkv_rows[:, part_index * feature_count:(part_index + 1) * feature_count]]
    ppermute x4 -> x12, starting transfers between devices: 5.31 us -> 33.1 us  [the longest x8 18.5 us: layer_backward(): lax.ppermute(item, 'section', owner_pairs)]
    another operation x25 -> x11, other arithmetic: 28.8 us -> 7.43 us  [the longest x6 6.38 us: on_device(): pairs = [jnp.stack([a, b]) for a, b in zip(own, other)]]
  transfers between devices with their start and end apart: 32 -> 36, of which waited for: 26 -> 17; matrix products, arithmetic and copies ran while one was open for 15% -> 14% of each run, Pallas kernels for 0% -> 0%
where the time goes in v1:
time: 1330 us; the launch traced here: 1320 us
  waiting for transfers between devices  734 us (55%)
  blocking collectives  207 us (16%)
  matrix products  148 us (11%)
  starting transfers between devices  75.5 us (6%)
  other arithmetic  73.7 us (6%)
  local copies, waits for them, and re-layouts  64.5 us (5%)
  between operations  16.2 us (1%)
    reduce_scatter x1, waiting for transfers between devices, on_device(): lax.psum_scatter(qkv_grad, chips, scatter_dimension=0, tiled=True)  156 us
    all_gather x3, blocking collectives, both_layers(): whole = lax.all_gather(shard, chips, axis=axis, tiled=True)  148 us
    all_gather x4, waiting for transfers between devices, to_experts(): return lax.all_gather(arrived, 'dp', axis=1, tiled=True)  145 us
    all_gather x2, waiting for transfers between devices, both_layers(): whole = lax.all_gather(shard, chips, axis=axis, tiled=True)  133 us
    reduce_scatter x1, waiting for transfers between devices, on_device(): lax.psum_scatter(out_grad, chips, scatter_dimension=0, tiled=True)  130 us
    all_to_all x4, waiting for transfers between devices, from_experts(): lax.all_to_all(partial.astype(half)[None], 'dp', split_axis=2, concat_axi...  93.2 us
    unnamed x15, waiting for transfers between devices  43.6 us
    all_to_all x4, blocking collectives, to_experts(): lax.all_to_all(blocks, 'expert', split_axis=0, concat_axis=1, tiled=True)  42.6 us
  transfers between devices with their start and end apart: 36, of which 17 were waited for; matrix products, arithmetic and copies ran while one was open for 14% of the time, Pallas kernels for 0%

profile of v1, /device:TPU:0, one launch (start us, length us, event | category | flops | bytes accessed | tf_op | source)
XLA Modules:
  0.0 1319.3 jit_solution(4148988462777251942)
XLA Ops:
  8.7 75.4 %all-gather.11.cloned.1.call-done = bf16[1,768,2304]{2,1,0:T(8,128)(2,1)} async-done(((bf16[1,48,2304]{2,1,0:T(8,128)(2,1)}), bf16[1,768,2304]{2,1,0:T(8,128)(2,1)}) %all-gather.11.cloned.1.call-update) | async-done | bytes 3538960 | tf_op jit(solution)/shard_map/all_gather | solution.py:124
  84.2 57.2 %all-gather.15.cloned.1.call-done = bf16[1,768,768]{2,1,0:T(8,128)(2,1)} async-done(((bf16[1,48,768]{2,1,0:T(8,128)(2,1)}), bf16[1,768,768]{2,1,0:T(8,128)(2,1)}) %all-gather.15.cloned.1.call-update) | async-done | bytes 1179664 | tf_op jit(solution)/shard_map/all_gather | solution.py:124
  146.5 40.7 %all_gather.50 = bf16[1,2,768]{1,0,2:T(2,128)(2,1)S(1)} all-gather(bf16[1,2,48]{1,0,2:T(2,128)(2,1)S(1)} %copy.152), channel_id=1, replica_groups=mesh['section'=2,'dp'=4,'expert'=4] {'dp','expert'}, dimensions={2}, use_global_device_ids=true | all-gather | bytes 3264 | tf_op jit(solution)/shard_map/all_gather | solution.py:124
  189.5 37.6 %all_gather.48 = bf16[1,2,768]{1,0,2:T(2,128)(2,1)S(1)} all-gather(bf16[1,2,48]{1,0,2:T(2,128)(2,1)S(1)} %copy.150), channel_id=1, replica_groups=mesh['section'=2,'dp'=4,'expert'=4] {'dp','expert'}, dimensions={2}, use_global_device_ids=true | all-gather | bytes 3264 | tf_op jit(solution)/shard_map/all_gather | solution.py:124
  252.3 11.6 all_to_all.201
  265.6 39.4 %all-gather.19.cloned.1.call-done = bf16[2,640,768]{2,1,0:T(8,128)(2,1)} async-done(((bf16[2,160,768]{2,1,0:T(8,128)(2,1)}), bf16[2,640,768]{2,1,0:T(8,128)(2,1)}) %all-gather.19.cloned.1.call-update) | async-done | bytes 1966096 | tf_op jit(solution)/shard_map/all_gather | solution.py:147
  311.8 9.9 fusion.6
  333.6 70.0 %all_gather.56 = bf16[1,768,8]{2,0,1:T(2,128)(2,1)S(1)} all-gather(bf16[1,48,8]{2,0,1:T(2,128)(2,1)S(1)} %copy.158), channel_id=1, replica_groups=mesh['section'=2,'dp'=4,'expert'=4] {'dp','expert'}, dimensions={1}, use_global_device_ids=true | all-gather | bytes 13056 | tf_op jit(solution)/shard_map/all_gather | solution.py:124
  415.1 7.9 all-to-all-done.5
  444.4 10.4 all_to_all.202
  459.6 9.4 all_to_all.203
  469.8 29.3 %all-gather.27.cloned.1.call-done = bf16[2,640,768]{2,1,0:T(8,128)(2,1)} async-done(((bf16[2,160,768]{2,1,0:T(8,128)(2,1)}), bf16[2,640,768]{2,1,0:T(8,128)(2,1)}) %all-gather.27.cloned.1.call-update) | async-done | bytes 1966096 | tf_op jit(solution)/shard_map/all_gather | solution.py:147
  499.1 7.8 fusion.96
  506.9 36.2 %all-gather.25.cloned.1.call-done = bf16[2,640,768]{2,1,0:T(8,128)(2,1)} async-done(((bf16[2,160,768]{2,1,0:T(8,128)(2,1)}), bf16[2,640,768]{2,1,0:T(8,128)(2,1)}) %all-gather.25.cloned.1.call-update) | async-done | bytes 1966096 | tf_op jit(solution)/shard_map/all_gather | solution.py:147
  561.1 10.3 fusion.15
  579.4 27.2 %all-to-all-done.8 = bf16[1,2,640,768]{3,1,0,2:T(2,128)(2,1)} async-done(((bf16[1,2,640,768]{3,1,0,2:T(2,128)(2,1)}), bf16[1,2,640,768]{3,1,0,2:T(2,128)(2,1)}, u32[]{:S(2)}, u32[]{:S(2)}) %all-to-all-start.8) | async-done | bytes 1966112 | tf_op jit(solution)/shard_map/all_to_all | solution.py:150
  615.7 40.3 %all-to-all-done.10 = bf16[1,2,640,768]{3,1,0,2:T(2,128)(2,1)} async-done(((bf16[1,2,640,768]{3,1,0,2:T(2,128)(2,1)}), bf16[1,2,640,768]{3,1,0,2:T(2,128)(2,1)}, u32[]{:S(2)}, u32[]{:S(2)}) %all-to-all-start.10) | async-done | bytes 1966112 | tf_op jit(solution)/shard_map/all_to_all | solution.py:150
  714.0 11.1 all_to_all.204
  726.0 40.4 %all-gather.29.cloned.1.call-done = bf16[2,640,768]{2,1,0:T(8,128)(2,1)} async-done(((bf16[2,160,768]{2,1,0:T(8,128)(2,1)}), bf16[2,640,768]{2,1,0:T(8,128)(2,1)}) %all-gather.29.cloned.1.call-update) | async-done | bytes 1966096 | tf_op jit(solution)/shard_map/all_gather | solution.py:147
  804.2 25.7 %all-to-all-done.13 = bf16[1,2,640,768]{3,1,0,2:T(2,128)(2,1)} async-done(((bf16[1,2,640,768]{3,1,0,2:T(2,128)(2,1)}), bf16[1,2,640,768]{3,1,0,2:T(2,128)(2,1)}, u32[]{:S(2)}, u32[]{:S(2)}) %all-to-all-start.13) | async-done | bytes 1966112 | tf_op jit(solution)/shard_map/all_to_all | solution.py:150
  877.5 16.2 %all-reduce.2.cloned.1.call-done = f32[2,12,768]{2,1,0:T(8,128)} async-done(((f32[2,12,768]{2,1,0:T(8,128)}), f32[2,12,768]{2,1,0:T(8,128)}) %all-reduce.2.cloned.1.call-update) | async-done | bytes 73744 | tf_op jit(solution)/shard_map/psum | solution.py:288
  981.1 41.3 %reduce-scatter.10.cloned.1.call-done = f32[48,12]{1,0:T(8,128)} async-done(((f32[768,12]{1,0:T(8,128)}), f32[48,12]{1,0:T(8,128)}) %reduce-scatter.10.cloned.1.call-update) | async-done | bytes 2320
  1026.1 130.0 %reduce-scatter.8.cloned.1.call-done = f32[48,768]{1,0:T(8,128)} async-done(((f32[768,768]{1,0:T(8,128)}), f32[48,768]{1,0:T(8,128)}) %reduce-scatter.8.cloned.1.call-update) | async-done | bytes 147472 | tf_op jit(solution)/shard_map/reduce_scatter | solution.py:292
  1156.1 156.2 %reduce-scatter.6.cloned.1.call-done = f32[48,2304]{1,0:T(8,128)} async-done(((f32[768,2304]{1,0:T(8,128)}), f32[48,2304]{1,0:T(8,128)}) %reduce-scatter.6.cloned.1.call-update) | async-done | bytes 442384 | tf_op jit(solution)/shard_map/reduce_scatter | solution.py:291
  (448 shorter events, 361.5 us)
Async XLA Ops:
  7.2 77.0 %all-gather.11.cloned.1.call-start = ((), (), s32[]{:S(2)}) async-start(), calls=%async_computation.19 | async-start | bytes 3760128 | tf_op jit(solution)/shard_map/all_gather | solution.py:124
  7.9 133.5 %all-gather.15.cloned.1.call-start = ((), (), s32[]{:S(2)}) async-start(), calls=%async_computation.21 | async-start | bytes 1253376 | tf_op jit(solution)/shard_map/all_gather | solution.py:124
  8.7 231.8 %all-gather.13.cloned.1.call-start = ((), (), s32[]{:S(2)}) async-start(), calls=%async_computation.20 | async-start | bytes 10616832 | tf_op jit(solution)/shard_map/all_gather | solution.py:125
  84.2 165.4 %all-gather.17.cloned.1.call-start = ((), (), s32[]{:S(2)}) async-start(), calls=%async_computation.22 | async-start | bytes 3538944 | tf_op jit(solution)/shard_map/all_gather | solution.py:125
  141.5 124.1 %all-gather.21.cloned.1.call-start = ((), (), s32[]{:S(2)}) async-start(), calls=%async_computation.24 | async-start | bytes 7077888 | tf_op jit(solution)/shard_map/all_gather | solution.py:132
  142.1 87.7 %all-to-all-start.1 = ((s32[2,197,2]{1,2,0:T(2,128)}), s32[2,197,2]{1,2,0:T(2,128)S(1)}, u32[]{:S(2)}, u32[]{:S(2)}) async-start(s32[2,197,2]{1,2,0:T(2,128)} %bitcast.11), calls=%async_computation.1 | async-start | bytes 8192 | tf_op jit(solution)/shard_map/all_to_all | solution.py:117
  237.1 67.9 %all-gather.19.cloned.1.call-start = ((), (), s32[]{:S(2)}) async-start(), calls=%async_computation.23 | async-start | bytes 2457600 | tf_op jit(solution)/shard_map/all_gather | solution.py:147
  264.8 56.9 %all-gather.23.cloned.1.call-start = ((), (), s32[]{:S(2)}) async-start(), calls=%async_computation.25 | async-start | bytes 7077888 | tf_op jit(solution)/shard_map/all_gather | solution.py:133
  328.9 77.6 %all-to-all-start.4 = ((bf16[1,2,640,768]{3,1,0,2:T(2,128)(2,1)}), bf16[1,2,640,768]{3,1,0,2:T(2,128)(2,1)}, u32[]{:S(2)}, u32[]{:S(2)}) async-start(bf16[1,2,640,768]{3,1,0,2:T(2,128)(2,1)} %copy.161), calls=%async_computation.4 | async-start | bytes 3932160 | tf_op jit(solution)/shard_map/all_to_all | solution.py:150
  414.8 84.4 %all-gather.27.cloned.1.call-start = ((), (), s32[]{:S(2)}) async-start(), calls=%async_computation.27 | async-start | bytes 2457600 | tf_op jit(solution)/shard_map/all_gather | solution.py:147
  455.6 87.4 %all-gather.25.cloned.1.call-start = ((), (), s32[]{:S(2)}) async-start(), calls=%async_computation.26 | async-start | bytes 2457600 | tf_op jit(solution)/shard_map/all_gather | solution.py:147
  556.4 50.2 %all-to-all-start.8 = ((bf16[1,2,640,768]{3,1,0,2:T(2,128)(2,1)}), bf16[1,2,640,768]{3,1,0,2:T(2,128)(2,1)}, u32[]{:S(2)}, u32[]{:S(2)}) async-start(bf16[1,2,640,768]{3,1,0,2:T(2,128)(2,1)} %copy.170), calls=%async_computation.8 | async-start | bytes 3932160 | tf_op jit(solution)/shard_map/all_to_all | solution.py:150
  606.6 49.5 %all-to-all-start.10 = ((bf16[1,2,640,768]{3,1,0,2:T(2,128)(2,1)}), bf16[1,2,640,768]{3,1,0,2:T(2,128)(2,1)}, u32[]{:S(2)}, u32[]{:S(2)}) async-start(bf16[1,2,640,768]{3,1,0,2:T(2,128)(2,1)} %copy.173), calls=%async_computation.10 | async-start | bytes 3932160 | tf_op jit(solution)/shard_map/all_to_all | solution.py:150
  671.6 94.8 %all-gather.29.cloned.1.call-start = ((), (), s32[]{:S(2)}) async-start(), calls=%async_computation.28 | async-start | bytes 2457600 | tf_op jit(solution)/shard_map/all_gather | solution.py:147
  779.8 50.1 %all-to-all-start.13 = ((bf16[1,2,640,768]{3,1,0,2:T(2,128)(2,1)}), bf16[1,2,640,768]{3,1,0,2:T(2,128)(2,1)}, u32[]{:S(2)}, u32[]{:S(2)}) async-start(bf16[1,2,640,768]{3,1,0,2:T(2,128)(2,1)} %copy.184), calls=%async_computation.13 | async-start | bytes 3932160 | tf_op jit(solution)/shard_map/all_to_all | solution.py:150
  786.9 89.5 %collective-permute-start.4 = (bf16[197,768]{1,0:T(8,128)(2,1)}, bf16[197,768]{1,0:T(8,128)(2,1)}, u32[]{:S(2)}, u32[]{:S(2)}) collective-permute-start(bf16[197,768]{1,0:T(8,128)(2,1)} %copy.200), channel_id=1, source_target_pairs={{16,0},{17,1},{18,2},{19,3},{20,4},{21,5},{22,6},{23,7},{24,8},{25... | collective-permute-start | bytes 907784 | tf_op jit(solution)/shard_map/ppermute | solution.py:254
  793.9 82.5 %collective-permute-start.5 = (bf16[197,768]{1,0:T(8,128)(2,1)}, bf16[197,768]{1,0:T(8,128)(2,1)}, u32[]{:S(2)}, u32[]{:S(2)}) collective-permute-start(bf16[197,768]{1,0:T(8,128)(2,1)} %copy.201), channel_id=1, source_target_pairs={{0,16},{1,17},{2,18},{3,19},{4,20},{5,21},{6,22},{7,23},{8,24},{9,... | collective-permute-start | bytes 907784 | tf_op jit(solution)/shard_map/ppermute | solution.py:254
  800.2 95.2 %collective-permute-start.7 = (bf16[197,768]{1,0:T(8,128)(2,1)}, bf16[197,768]{1,0:T(8,128)(2,1)}, u32[]{:S(2)}, u32[]{:S(2)}) collective-permute-start(bf16[197,768]{1,0:T(8,128)(2,1)} %copy-done.43), channel_id=1, source_target_pairs={{0,16},{1,17},{2,18},{3,19},{4,20},{5,21},{6,22},{7,23},{8,24},{9,... | collective-permute-start | bytes 907784 | tf_op jit(solution)/shard_map/ppermute | solution.py:254
  838.4 55.2 %all-reduce.2.cloned.1.call-start = ((), (), s32[]{:S(2)}) async-start(), calls=%async_computation.29 | async-start | bytes 196608 | tf_op jit(solution)/shard_map/psum | solution.py:288
  868.2 27.3 %collective-permute-start.6 = (bf16[197,768]{1,0:T(8,128)(2,1)}, bf16[197,768]{1,0:T(8,128)(2,1)}, u32[]{:S(2)}, u32[]{:S(2)}) collective-permute-start(bf16[197,768]{1,0:T(8,128)(2,1)} %copy-done.51), channel_id=1, source_target_pairs={{16,0},{17,1},{18,2},{19,3},{20,4},{21,5},{22,6},{23,7},{24,8},{25... | collective-permute-start | bytes 907784 | tf_op jit(solution)/shard_map/ppermute | solution.py:254
  876.4 146.1 %reduce-scatter.10.cloned.1.call-start = ((), (), s32[]{:S(2)}) async-start(), calls=%async_computation.32 | async-start | bytes 417792
  895.4 260.6 %reduce-scatter.8.cloned.1.call-start = ((), (), s32[]{:S(2)}) async-start(), calls=%async_computation.31 | async-start | bytes 2506752 | tf_op jit(solution)/shard_map/reduce_scatter | solution.py:292
  898.9 413.4 %reduce-scatter.6.cloned.1.call-start = ((), (), s32[]{:S(2)}) async-start(), calls=%async_computation.30 | async-start | bytes 7520256 | tf_op jit(solution)/shard_map/reduce_scatter | solution.py:291
  933.0 25.4 %collective-permute-start.9 = (bf16[2,768,768]{2,1,0:T(8,128)(2,1)S(1)}, bf16[2,768,768]{2,1,0:T(8,128)(2,1)}, u32[]{:S(2)}, u32[]{:S(2)}) collective-permute-start(bf16[2,768,768]{2,1,0:T(8,128)(2,1)S(1)} %get-tuple-element.113), channel_id=1, source_target_pairs={{0,16},{1,17},{2,18},{3,19},{4,20},{5,21},{6,22},{7,23},{8,24},{9,... | collective-permute-start | bytes 7077896 | tf_op jit(solution)/shard_map/ppermute | solution.py:225
  (109 other events, 1345.8 us)
Sparse Core Ops, SparseCore 0:
  10.8 73.3 all-gather.10
  86.9 54.4 all-gather.14
  143.0 16.6 all-gather.12
  161.0 12.1 all-gather.16
  174.6 15.6 all-gather.20
  264.9 40.0 all-gather.18
  306.6 13.2 all-gather.22
  455.7 43.3 all-gather.26
  500.7 42.3 all-gather.24
  726.1 40.2 all-gather.28
  876.5 17.0 all-reduce.1
  898.1 124.2 reduce-scatter.9
  1027.9 128.0 reduce-scatter.7
  1161.8 150.4 reduce-scatter.5

commit v2 on v1

--- a/solution.py
+++ b/solution.py
@@ -105,7 +105,9 @@
 ):
     section_index = lax.axis_index("section")
     is_first = section_index == 0
-    expert_count = EXP_DEV * lax.axis_size("expert")
+    depth = lax.axis_size("dp")
+    groups = lax.axis_size("expert")
+    expert_count = EXP_DEV * groups
     local_images = boundary_in.shape[2]
     token_rows = local_images * boundary_in.shape[3]
     model_width = boundary_in.shape[4]
@@ -120,15 +122,19 @@
     route_rows = by_micro(routes[0].reshape(MB, token_rows, 2))
     slot_rows = by_micro(capacity_slots[0].reshape(MB, token_rows, 2))
 
-    def both_layers(shard, axis):
-        whole = lax.all_gather(shard, chips, axis=axis, tiled=True)
-        return lax.all_gather(whole, "section", axis=0, tiled=True)
-
-    gain_all = both_layers(ln_gain, 2).astype(jnp.float32)
-    shift_all = both_layers(ln_bias, 2).astype(jnp.float32)
-    qkv_all = both_layers(w_qkv, 1)
-    out_all = both_layers(w_out, 1)
-    router_all = both_layers(w_router, 1)
+    norm_columns = jnp.concatenate([ln_gain, ln_bias], axis=1).transpose(0, 2, 1)
+    used = 4 * model_width + expert_count + 4
+    padding = -used % 128
+    packed = jnp.concatenate([w_qkv, w_out, w_router, norm_columns], axis=2)
+    packed = jnp.pad(packed, ((0, 0), (0, 0), (0, padding)))
+    packed = lax.all_gather(packed, chips, axis=1, tiled=True)
+    packed = lax.all_gather(packed, "section", axis=0, tiled=True)
+    qkv_all = packed[:, :, : 3 * model_width]
+    out_all = packed[:, :, 3 * model_width : 4 * model_width]
+    router_all = packed[:, :, 4 * model_width : used - 4]
+    norm_all = packed[:, :, used - 4 : used].transpose(0, 2, 1).astype(jnp.float32)
+    gain_all = norm_all[:, 0:2]
+    shift_all = norm_all[:, 2:4]
     up_all = lax.all_gather(w_up, "section", axis=0, tiled=True)
     down_all = lax.all_gather(w_down, "section", axis=0, tiled=True)
 
@@ -147,12 +153,14 @@
         return lax.all_gather(arrived, "dp", axis=1, tiled=True)
 
     def from_experts(partial):
+        chunks = partial.astype(half).reshape(EXP_DEV, depth, -1, model_width)
         pieces = lax.all_to_all(
-            partial.astype(half)[None], "dp", split_axis=2, concat_axis=0, tiled=True
+            chunks.transpose(1, 0, 2, 3), "dp", split_axis=0, concat_axis=0, tiled=True
         )
         total = jnp.sum(pieces.astype(jnp.float32), axis=0).astype(half)
+        blocks = total.reshape(EXP_DEV, groups, capacity, model_width).transpose(1, 0, 2, 3)
         return lax.all_to_all(
-            total, "expert", split_axis=1, concat_axis=0, tiled=True
+            blocks, "expert", split_axis=0, concat_axis=0, tiled=True
         ).reshape(expert_count * capacity, model_width)
 
     def layer_forward(layer, inputs):
@@ -257,10 +265,12 @@
         own = (norm_one, d_qkv, attended, d_middle_half)
         small = jnp.concatenate(
             [
+                jnp.einsum("td,te->ed", norm_two, d_logits, preferred_element_type=jnp.float32),
                 jnp.stack([gain_one, gain_two, shift_one, shift_two]),
-                jnp.einsum("td,te->ed", norm_two, d_logits, preferred_element_type=jnp.float32),
             ]
         )
+        small_sent = lax.ppermute(small, "section", owner_pairs)
+        small = small + small_sent
         return (d_input, own, operands, small, (up_grad, up_sent), (down_grad, down_sent))
 
     stream = edge_rows[0]
@@ -285,11 +295,17 @@
     pairs = [jnp.stack([a, b]) for a, b in zip(own, other)]
     qkv_grad = jnp.einsum("ktd,kte->de", pairs[0], pairs[1], preferred_element_type=jnp.float32)
     out_grad = jnp.einsum("ktd,kte->de", pairs[2], pairs[3], preferred_element_type=jnp.float32)
-    small_both = lax.psum(jnp.stack([parts[0][2], parts[1][2]]), "section")
-    small_mine = mine(small_both[0], small_both[1])
-    small_shard = lax.psum_scatter(small_mine, chips, scatter_dimension=1, tiled=True)
-    qkv_shard = lax.psum_scatter(qkv_grad, chips, scatter_dimension=0, tiled=True)
-    out_shard = lax.psum_scatter(out_grad, chips, scatter_dimension=0, tiled=True)
+    small_mine = mine(parts[0][2], parts[1][2])
+
+    packed_grad = jnp.concatenate(
+        [qkv_grad, out_grad, small_mine.T, jnp.zeros((model_width, padding), jnp.float32)], axis=1
+    ).astype(half)
+    blocks = packed_grad.reshape(depth, groups, -1, packed_grad.shape[1]).transpose(1, 0, 2, 3)
+    blocks = lax.all_to_all(blocks, "expert", split_axis=0, concat_axis=0, tiled=True)
+    blocks = jnp.sum(blocks.astype(jnp.float32), axis=0).astype(half)
+    blocks = lax.all_to_all(blocks, "dp", split_axis=0, concat_axis=0, tiled=True)
+    grad_shard = jnp.sum(blocks.astype(jnp.float32), axis=0)
+    norm_shard = grad_shard[:, used - 4 : used].T
 
     def expert_grad(index):
         first = parts[0][index][0] + parts[0][index][1].astype(jnp.float32)
@@ -298,15 +314,17 @@
 
     up_shard = expert_grad(3)
     down_shard = expert_grad(4)
-    boundary_rows = by_micro(jnp.stack([cotangent, stream]))
+    out_sent = lax.ppermute(stream, "section", [(0, 1)])
+    grad_sent = lax.ppermute(cotangent, "section", [(1, 0)])
+    boundary_rows = mine(jnp.stack([cotangent, grad_sent]), jnp.stack([out_sent, stream]))
     boundary_out = boundary_rows.reshape(1, MB, local_images, boundary_in.shape[3], model_width)
     return (
         boundary_out,
-        small_shard[None, 0:2],
-        small_shard[None, 2:4],
-        qkv_shard[None],
-        out_shard[None],
-        small_shard[4:].T[None],
+        norm_shard[None, 0:2],
+        norm_shard[None, 2:4],
+        grad_shard[None, :, : 3 * model_width],
+        grad_shard[None, :, 3 * model_width : 4 * model_width],
+        grad_shard[None, :, 4 * model_width : used - 4],
         up_shard,
         down_shard,
     )

time: 1330 us -> 866 us (0.65)
  waiting for transfers between devices: 734 us -> 400 us
  blocking collectives: 207 us -> 45.7 us
  starting transfers between devices: 75.5 us -> 104 us
    reduce_scatter x2 -> x0, waiting for transfers between devices: 286 us -> none  [the longest x1 156 us: on_device(): lax.psum_scatter(qkv_grad, chips, scatter_dimension=0, tiled=True)]
    all_gather x6 -> x0, blocking collectives: 154 us -> none  [the longest x3 148 us: both_layers(): whole = lax.all_gather(shard, chips, axis=axis, tiled=True)]
    all_to_all x8 -> x10, waiting for transfers between devices: 108 us -> 160 us  [the longest x4 119 us: from_experts(): lax.all_to_all(chunks.transpose(1, 0, 2, 3), 'dp', split_axis=0, concat_a...]
    unnamed x15 -> x8, waiting for transfers between devices: 43.6 us -> 1.31 us
    all_gather x4 -> x2, waiting for transfers between devices: 133 us -> 91 us  [the longest x1 84.9 us: on_device(): packed = lax.all_gather(packed, chips, axis=1, tiled=True)]
    all_to_all x8 -> x10, starting transfers between devices: 33.7 us -> 53.7 us  [the longest x4 29.5 us: from_experts(): lax.all_to_all(chunks.transpose(1, 0, 2, 3), 'dp', split_axis=0, concat_a...]
    psum x1 -> x0, waiting for transfers between devices: 16.2 us -> none  [on_device(): small_both = lax.psum(jnp.stack([parts[0][2], parts[1][2]]), 'section')]
  transfers between devices with their start and end apart: 36 -> 36, of which waited for: 17 -> 19; matrix products, arithmetic and copies ran while one was open for 14% -> 21% of each run, Pallas kernels for 0% -> 0%
where the time goes in v2:
time: 866 us; the launch traced here: 860 us
  waiting for transfers between devices  400 us (46%)
  matrix products  156 us (18%)
  starting transfers between devices  104 us (12%)
  other arithmetic  75 us (9%)
  local copies, waits for them, and re-layouts  62.4 us (7%)
  blocking collectives  45.7 us (5%)
  between operations  16 us (2%)
    all_gather x4, waiting for transfers between devices, to_experts(): return lax.all_gather(arrived, 'dp', axis=1, tiled=True)  145 us
    all_to_all x4, waiting for transfers between devices, from_experts(): lax.all_to_all(chunks.transpose(1, 0, 2, 3), 'dp', split_axis=0, concat_a...  119 us
    all_gather x1, waiting for transfers between devices, on_device(): packed = lax.all_gather(packed, chips, axis=1, tiled=True)  84.9 us
    all_to_all x4, blocking collectives, to_experts(): lax.all_to_all(blocks, 'expert', split_axis=0, concat_axis=1, tiled=True)  42 us
    all_to_all x4, starting transfers between devices, from_experts(): lax.all_to_all(chunks.transpose(1, 0, 2, 3), 'dp', split_axis=0, concat_a...  29.5 us
    convert_element_type x2, other arithmetic, layer_forward(): hidden = jax.nn.gelu(pre_act, approximate=False).astype(half)  20.2 us
    ppermute x8, starting transfers between devices, layer_backward(): lax.ppermute(item, 'section', owner_pairs)  18.8 us
  transfers between devices with their start and end apart: 36, of which 19 were waited for; matrix products, arithmetic and copies ran while one was open for 21% of the time, Pallas kernels for 0%

profile of v2, /device:TPU:0, one launch (start us, length us, event | category | flops | bytes accessed | tf_op | source)
XLA Modules:
  0.0 859.7 jit_solution(10643462404687970666)
XLA Ops:
  10.7 84.9 %all-gather.9.cloned.1.call-done = bf16[1,768,3200]{2,1,0:T(8,128)(2,1)} async-done(((bf16[1,48,3200]{2,1,0:T(8,128)(2,1)}), bf16[1,768,3200]{2,1,0:T(8,128)(2,1)}) %all-gather.9.cloned.1.call-update) | async-done | bytes 4915216 | tf_op jit(solution)/shard_map/all_gather | solution.py:130
  111.7 6.1 all-gather.11.cloned.1.call-done
  133.2 12.4 %all_to_all.138 = bf16[8,40,768]{2,1,0:T(8,128)(2,1)S(1)} all-to-all(bf16[8,40,768]{2,1,0:T(8,128)(2,1)S(1)} %bitcast.390), channel_id=1, replica_groups=mesh['section'=2,'dp'=4,'expert'=4] {'expert'}, dimensions={0} | all-to-all | bytes 983040 | tf_op jit(solution)/shard_map/all_to_all | solution.py:152
  147.1 42.4 %all-gather.13.cloned.1.call-done = bf16[2,640,768]{2,1,0:T(8,128)(2,1)} async-done(((bf16[2,160,768]{2,1,0:T(8,128)(2,1)}), bf16[2,640,768]{2,1,0:T(8,128)(2,1)}) %all-gather.13.cloned.1.call-update) | async-done | bytes 1966096 | tf_op jit(solution)/shard_map/all_gather | solution.py:153
  196.2 9.9 %fusion.6 = bf16[2,640,768]{2,1,0:T(8,128)(2,1)} fusion(f32[2,640,768]{2,1,0:T(8,128)S(1)} %get-tuple-element.109, u8[640,768]{1,0:T(8,128)(4,1)S(1)} %get-tuple-element.51, u8[640,768]{1,0:T(8,128)(4,1)S(1)} %get-tuple-element.50), kind=kLoop, calls=%fused_computation.13 | loop fusion | flops 68812800 | bytes 6881280 | tf_op jit(solution)/shard_map/convert_element_type | solution.py:190
  217.9 43.7 %all-to-all-done.4 = bf16[4,2,160,768]{3,2,1,0:T(8,128)(2,1)} async-done(((bf16[4,2,160,768]{3,2,1,0:T(8,128)(2,1)}), bf16[4,2,160,768]{3,2,1,0:T(8,128)(2,1)}, u32[]{:S(2)}, u32[]{:S(2)}) %all-to-all-start.4) | async-done | bytes 1966112 | tf_op jit(solution)/shard_map/all_to_all | solution.py:157
  268.3 6.9 all-to-all-done.5
  297.2 9.6 %all_to_all.139 = bf16[8,40,768]{2,1,0:T(8,128)(2,1)S(1)} all-to-all(bf16[8,40,768]{2,1,0:T(8,128)(2,1)S(1)} %bitcast.391), channel_id=1, replica_groups=mesh['section'=2,'dp'=4,'expert'=4] {'expert'}, dimensions={0} | all-to-all | bytes 983040 | tf_op jit(solution)/shard_map/all_to_all | solution.py:152
  311.8 9.4 %all_to_all.140 = bf16[8,40,768]{2,1,0:T(8,128)(2,1)S(1)} all-to-all(bf16[8,40,768]{2,1,0:T(8,128)(2,1)S(1)} %bitcast.429), channel_id=1, replica_groups=mesh['section'=2,'dp'=4,'expert'=4] {'expert'}, dimensions={0} | all-to-all | bytes 983040 | tf_op jit(solution)/shard_map/all_to_all | solution.py:152
  322.1 26.3 %all-gather.21.cloned.1.call-done = bf16[2,640,768]{2,1,0:T(8,128)(2,1)} async-done(((bf16[2,160,768]{2,1,0:T(8,128)(2,1)}), bf16[2,640,768]{2,1,0:T(8,128)(2,1)}) %all-gather.21.cloned.1.call-update) | async-done | bytes 1966096 | tf_op jit(solution)/shard_map/all_gather | solution.py:153
  348.4 7.7 fusion.100
  356.1 36.2 %all-gather.19.cloned.1.call-done = bf16[2,640,768]{2,1,0:T(8,128)(2,1)} async-done(((bf16[2,160,768]{2,1,0:T(8,128)(2,1)}), bf16[2,640,768]{2,1,0:T(8,128)(2,1)}) %all-gather.19.cloned.1.call-update) | async-done | bytes 1966096 | tf_op jit(solution)/shard_map/all_gather | solution.py:153
  403.2 15.9 %all-to-all-start.8 = ((bf16[4,2,160,768]{3,2,1,0:T(8,128)(2,1)}), bf16[4,2,160,768]{3,2,1,0:T(8,128)(2,1)}, u32[]{:S(2)}, u32[]{:S(2)}) async-start(bf16[4,2,160,768]{3,2,1,0:T(8,128)(2,1)} %bitcast.369), calls=%async_computation.8 | async-start | bytes 3932160 | tf_op jit(solution)/shard_map/all_to_all | solution.py:157
  419.1 10.3 %fusion.15 = bf16[2,640,768]{2,1,0:T(8,128)(2,1)S(1)} fusion(f32[2,640,768]{2,1,0:T(8,128)} %get-tuple-element.114, u8[640,768]{1,0:T(8,128)(4,1)} %get-tuple-element.49, u8[640,768]{1,0:T(8,128)(4,1)} %get-tuple-element.48), kind=kLoop, calls=%fused_computation.22 | loop fusion | flops 68812800 | bytes 6881280 | tf_op jit(solution)/shard_map/convert_element_type | solution.py:190
  435.0 29.4 %all-to-all-done.8 = bf16[4,2,160,768]{3,2,1,0:T(8,128)(2,1)} async-done(((bf16[4,2,160,768]{3,2,1,0:T(8,128)(2,1)}), bf16[4,2,160,768]{3,2,1,0:T(8,128)(2,1)}, u32[]{:S(2)}, u32[]{:S(2)}) %all-to-all-start.8) | async-done | bytes 1966112 | tf_op jit(solution)/shard_map/all_to_all | solution.py:157
  473.4 40.4 %all-to-all-done.10 = bf16[4,2,160,768]{3,2,1,0:T(8,128)(2,1)} async-done(((bf16[4,2,160,768]{3,2,1,0:T(8,128)(2,1)}), bf16[4,2,160,768]{3,2,1,0:T(8,128)(2,1)}, u32[]{:S(2)}, u32[]{:S(2)}) %all-to-all-start.10) | async-done | bytes 1966112 | tf_op jit(solution)/shard_map/all_to_all | solution.py:157
  572.9 10.6 %all_to_all.141 = bf16[8,40,768]{2,1,0:T(8,128)(2,1)S(1)} all-to-all(bf16[8,40,768]{2,1,0:T(8,128)(2,1)S(1)} %bitcast.428), channel_id=1, replica_groups=mesh['section'=2,'dp'=4,'expert'=4] {'expert'}, dimensions={0} | all-to-all | bytes 983040 | tf_op jit(solution)/shard_map/all_to_all | solution.py:152
  584.3 40.4 %all-gather.23.cloned.1.call-done = bf16[2,640,768]{2,1,0:T(8,128)(2,1)} async-done(((bf16[2,160,768]{2,1,0:T(8,128)(2,1)}), bf16[2,640,768]{2,1,0:T(8,128)(2,1)}) %all-gather.23.cloned.1.call-update) | async-done | bytes 1966096 | tf_op jit(solution)/shard_map/all_gather | solution.py:153
  692.3 6.8 all-to-all-done.14
  741.9 7.6 concatenate.94
  754.5 7.3 fusion.227
  796.8 13.4 %all-to-all-done.15 = bf16[4,4,48,3200]{3,2,1,0:T(8,128)(2,1)} async-done(((bf16[4,4,48,3200]{3,2,1,0:T(8,128)(2,1)}), bf16[4,4,48,3200]{3,2,1,0:T(8,128)(2,1)}, u32[]{:S(2)}, u32[]{:S(2)}) %all-to-all-start.15) | async-done | bytes 4915232 | tf_op jit(solution)/shard_map/all_to_all | solution.py:304
  818.4 8.6 select_bitcast_fusion.1
  837.7 11.2 %all-to-all-done.16 = bf16[4,48,3200]{2,1,0:T(8,128)(2,1)S(1)} async-done(((bf16[4,48,3200]{2,1,0:T(8,128)(2,1)}), bf16[4,48,3200]{2,1,0:T(8,128)(2,1)S(1)}, u32[]{:S(2)}, u32[]{:S(2)}) %all-to-all-start.16) | async-done | bytes 1228832 | tf_op jit(solution)/shard_map/all_to_all | solution.py:306
  (401 shorter events, 346.3 us)
Async XLA Ops:
  7.2 88.4 %all-gather.9.cloned.1.call-start = ((), (), s32[]{:S(2)}) async-start(), calls=%async_computation.17 | async-start | bytes 5222400 | tf_op jit(solution)/shard_map/all_gather | solution.py:130
  10.6 107.2 %all-gather.11.cloned.1.call-start = ((), (), s32[]{:S(2)}) async-start(), calls=%async_computation.18 | async-start | bytes 14745600 | tf_op jit(solution)/shard_map/all_gather | solution.py:131
  95.6 51.5 %all-gather.15.cloned.1.call-start = ((), (), s32[]{:S(2)}) async-start(), calls=%async_computation.20 | async-start | bytes 7077888 | tf_op jit(solution)/shard_map/all_gather | solution.py:138
  108.4 81.1 %all-gather.13.cloned.1.call-start = ((), (), s32[]{:S(2)}) async-start(), calls=%async_computation.19 | async-start | bytes 2457600 | tf_op jit(solution)/shard_map/all_gather | solution.py:153
  146.4 59.7 %all-gather.17.cloned.1.call-start = ((), (), s32[]{:S(2)}) async-start(), calls=%async_computation.21 | async-start | bytes 7077888 | tf_op jit(solution)/shard_map/all_gather | solution.py:139
  211.4 50.2 %all-to-all-start.4 = ((bf16[4,2,160,768]{3,2,1,0:T(8,128)(2,1)}), bf16[4,2,160,768]{3,2,1,0:T(8,128)(2,1)}, u32[]{:S(2)}, u32[]{:S(2)}) async-start(bf16[4,2,160,768]{3,2,1,0:T(8,128)(2,1)} %bitcast.367), calls=%async_computation.4 | async-start | bytes 3932160 | tf_op jit(solution)/shard_map/all_to_all | solution.py:157
  268.2 80.1 %all-gather.21.cloned.1.call-start = ((), (), s32[]{:S(2)}) async-start(), calls=%async_computation.23 | async-start | bytes 2457600 | tf_op jit(solution)/shard_map/all_gather | solution.py:153
  307.6 84.7 %all-gather.19.cloned.1.call-start = ((), (), s32[]{:S(2)}) async-start(), calls=%async_computation.22 | async-start | bytes 2457600 | tf_op jit(solution)/shard_map/all_gather | solution.py:153
  403.2 61.2 %all-to-all-start.8 = ((bf16[4,2,160,768]{3,2,1,0:T(8,128)(2,1)}), bf16[4,2,160,768]{3,2,1,0:T(8,128)(2,1)}, u32[]{:S(2)}, u32[]{:S(2)}) async-start(bf16[4,2,160,768]{3,2,1,0:T(8,128)(2,1)} %bitcast.369), calls=%async_computation.8 | async-start | bytes 3932160 | tf_op jit(solution)/shard_map/all_to_all | solution.py:157
  464.4 49.4 %all-to-all-start.10 = ((bf16[4,2,160,768]{3,2,1,0:T(8,128)(2,1)}), bf16[4,2,160,768]{3,2,1,0:T(8,128)(2,1)}, u32[]{:S(2)}, u32[]{:S(2)}) async-start(bf16[4,2,160,768]{3,2,1,0:T(8,128)(2,1)} %bitcast.368), calls=%async_computation.10 | async-start | bytes 3932160 | tf_op jit(solution)/shard_map/all_to_all | solution.py:157
  529.4 95.3 %all-gather.23.cloned.1.call-start = ((), (), s32[]{:S(2)}) async-start(), calls=%async_computation.24 | async-start | bytes 2457600 | tf_op jit(solution)/shard_map/all_gather | solution.py:153
  635.6 50.1 %all-to-all-start.13 = ((bf16[4,2,160,768]{3,2,1,0:T(8,128)(2,1)}), bf16[4,2,160,768]{3,2,1,0:T(8,128)(2,1)}, u32[]{:S(2)}, u32[]{:S(2)}) async-start(bf16[4,2,160,768]{3,2,1,0:T(8,128)(2,1)} %bitcast.366), calls=%async_computation.13 | async-start | bytes 3932160 | tf_op jit(solution)/shard_map/all_to_all | solution.py:157
  642.1 21.1 %collective-permute-start.6 = (bf16[197,768]{1,0:T(8,128)(2,1)}, bf16[197,768]{1,0:T(8,128)(2,1)}, u32[]{:S(2)}, u32[]{:S(2)}) collective-permute-start(bf16[197,768]{1,0:T(8,128)(2,1)} %copy.264), channel_id=1, source_target_pairs={{16,0},{17,1},{18,2},{19,3},{20,4},{21,5},{22,6},{23,7},{24,8},{25... | collective-permute-start | bytes 907784 | tf_op jit(solution)/shard_map/ppermute | solution.py:262
  643.4 18.1 %collective-permute-start.3 = (bf16[197,768]{1,0:T(8,128)(2,1)}, bf16[197,768]{1,0:T(8,128)(2,1)}, u32[]{:S(2)}, u32[]{:S(2)}) collective-permute-start(bf16[197,768]{1,0:T(8,128)(2,1)} %copy-done.38), channel_id=1, source_target_pairs={{0,16},{1,17},{2,18},{3,19},{4,20},{5,21},{6,22},{7,23},{8,24},{9,... | collective-permute-start | bytes 907784 | tf_op jit(solution)/shard_map/ppermute | solution.py:262
  665.0 69.3 %collective-permute-start.9 = (bf16[197,768]{1,0:T(8,128)(2,1)}, bf16[197,768]{1,0:T(8,128)(2,1)}, u32[]{:S(2)}, u32[]{:S(2)}) collective-permute-start(bf16[197,768]{1,0:T(8,128)(2,1)} %copy-done.30), channel_id=1, source_target_pairs={{0,16},{1,17},{2,18},{3,19},{4,20},{5,21},{6,22},{7,23},{8,24},{9,... | collective-permute-start | bytes 907784 | tf_op jit(solution)/shard_map/ppermute | solution.py:262
  669.1 67.2 %collective-permute-start.5 = (bf16[197,2304]{1,0:T(8,128)(2,1)}, bf16[197,2304]{1,0:T(8,128)(2,1)}, u32[]{:S(2)}, u32[]{:S(2)}) collective-permute-start(bf16[197,2304]{1,0:T(8,128)(2,1)} %pad_maximum_fusion), channel_id=1, source_target_pairs={{0,16},{1,17},{2,18},{3,19},{4,20},{5,21},{6,22},{7,23},{8,24},{9,... | collective-permute-start | bytes 2723336 | tf_op jit(solution)/shard_map/ppermute | solution.py:262
  676.2 52.1 %collective-permute-start.11 = (f32[12,768]{1,0:T(8,128)S(1)}, f32[12,768]{1,0:T(8,128)}, u32[]{:S(2)}, u32[]{:S(2)}) collective-permute-start(f32[12,768]{1,0:T(8,128)S(1)} %concatenate.92), channel_id=1, source_target_pairs={{0,16},{1,17},{2,18},{3,19},{4,20},{5,21},{6,22},{7,23},{8,24},{9,... | collective-permute-start | bytes 110600 | tf_op jit(solution)/shard_map/ppermute | solution.py:272
  749.5 60.7 %all-to-all-start.15 = ((bf16[4,4,48,3200]{3,2,1,0:T(8,128)(2,1)}), bf16[4,4,48,3200]{3,2,1,0:T(8,128)(2,1)}, u32[]{:S(2)}, u32[]{:S(2)}) async-start(bf16[4,4,48,3200]{3,2,1,0:T(8,128)(2,1)} %bitcast.361), calls=%async_computation.15 | async-start | bytes 9830400 | tf_op jit(solution)/shard_map/all_to_all | solution.py:304
  761.8 56.5 %collective-permute-start.13 = (bf16[2,768,768]{2,1,0:T(8,128)(2,1)}, bf16[2,768,768]{2,1,0:T(8,128)(2,1)}, u32[]{:S(2)}, u32[]{:S(2)}) collective-permute-start(bf16[2,768,768]{2,1,0:T(8,128)(2,1)} %get-tuple-element.121), channel_id=1, source_target_pairs={{0,16},{1,17},{2,18},{3,19},{4,20},{5,21},{6,22},{7,23},{8,24},{9,... | collective-permute-start | bytes 7077896 | tf_op jit(solution)/shard_map/ppermute | solution.py:233
  772.3 46.0 %collective-permute-start.12 = (bf16[2,768,768]{2,1,0:T(8,128)(2,1)}, bf16[2,768,768]{2,1,0:T(8,128)(2,1)}, u32[]{:S(2)}, u32[]{:S(2)}) collective-permute-start(bf16[2,768,768]{2,1,0:T(8,128)(2,1)} %get-tuple-element.123), channel_id=1, source_target_pairs={{16,0},{17,1},{18,2},{19,3},{20,4},{21,5},{22,6},{23,7},{24,8},{25... | collective-permute-start | bytes 7077896 | tf_op jit(solution)/shard_map/ppermute | solution.py:233
  779.2 49.3 %collective-permute-start.15 = (bf16[2,768,768]{2,1,0:T(8,128)(2,1)}, bf16[2,768,768]{2,1,0:T(8,128)(2,1)}, u32[]{:S(2)}, u32[]{:S(2)}) collective-permute-start(bf16[2,768,768]{2,1,0:T(8,128)(2,1)} %get-tuple-element.125), channel_id=1, source_target_pairs={{0,16},{1,17},{2,18},{3,19},{4,20},{5,21},{6,22},{7,23},{8,24},{9,... | collective-permute-start | bytes 7077896 | tf_op jit(solution)/shard_map/ppermute | solution.py:234
  790.3 38.3 %collective-permute-start.14 = (bf16[2,768,768]{2,1,0:T(8,128)(2,1)}, bf16[2,768,768]{2,1,0:T(8,128)(2,1)}, u32[]{:S(2)}, u32[]{:S(2)}) collective-permute-start(bf16[2,768,768]{2,1,0:T(8,128)(2,1)} %get-tuple-element.127), channel_id=1, source_target_pairs={{16,0},{17,1},{18,2},{19,3},{20,4},{21,5},{22,6},{23,7},{24,8},{25... | collective-permute-start | bytes 7077896 | tf_op jit(solution)/shard_map/ppermute | solution.py:234
  791.5 42.5 %collective-permute-start.1 = (f32[197,768]{1,0:T(8,128)}, f32[197,768]{1,0:T(8,128)}, u32[]{:S(2)}, u32[]{:S(2)}) collective-permute-start(f32[197,768]{1,0:T(8,128)} %get-tuple-element.100), channel_id=1, source_target_pairs={{0,16},{1,17},{2,18},{3,19},{4,20},{5,21},{6,22},{7,23},{8,24},{9,... | collective-permute-start | bytes 1815560 | tf_op jit(solution)/shard_map/ppermute | solution.py:317
  814.7 34.2 %all-to-all-start.16 = ((bf16[4,48,3200]{2,1,0:T(8,128)(2,1)}), bf16[4,48,3200]{2,1,0:T(8,128)(2,1)S(1)}, u32[]{:S(2)}, u32[]{:S(2)}) async-start(bf16[4,48,3200]{2,1,0:T(8,128)(2,1)} %reduce_sum.473), calls=%async_computation.16 | async-start | bytes 2457600 | tf_op jit(solution)/shard_map/all_to_all | solution.py:306
  (90 other events, 1006.6 us)
Sparse Core Ops, SparseCore 0:
  11.3 84.1 all-gather.8
  97.1 20.6 all-gather.10
  119.4 15.6 all-gather.14
  146.6 42.8 all-gather.12
  190.8 13.2 all-gather.16
  307.7 40.6 all-gather.20
  349.9 42.3 all-gather.18
  584.4 40.2 all-gather.22

commit v3 on v2

--- a/solution.py
+++ b/solution.py
@@ -127,14 +127,20 @@
     padding = -used % 128
     packed = jnp.concatenate([w_qkv, w_out, w_router, norm_columns], axis=2)
     packed = jnp.pad(packed, ((0, 0), (0, 0), (0, padding)))
-    packed = lax.all_gather(packed, chips, axis=1, tiled=True)
-    packed = lax.all_gather(packed, "section", axis=0, tiled=True)
-    qkv_all = packed[:, :, : 3 * model_width]
-    out_all = packed[:, :, 3 * model_width : 4 * model_width]
-    router_all = packed[:, :, 4 * model_width : used - 4]
-    norm_all = packed[:, :, used - 4 : used].transpose(0, 2, 1).astype(jnp.float32)
-    gain_all = norm_all[:, 0:2]
-    shift_all = norm_all[:, 2:4]
+    halves = by_micro(packed[0].reshape(2, -1, packed.shape[2]))
+    qkv_all, out_all, router_all, gain_all, shift_all = [], [], [], [], []
+
+    def gather_layer(shard):
+        part = lax.all_gather(shard[None], chips, axis=0, tiled=True)
+        whole = lax.all_gather(part, "section", axis=1).reshape(model_width, -1)
+        norm_rows = whole[:, used - 4 : used].T.astype(jnp.float32)
+        qkv_all.append(whole[:, : 3 * model_width])
+        out_all.append(whole[:, 3 * model_width : 4 * model_width])
+        router_all.append(whole[:, 4 * model_width : used - 4])
+        gain_all.append(norm_rows[0:2])
+        shift_all.append(norm_rows[2:4])
+
+    gather_layer(halves[0])
     up_all = lax.all_gather(w_up, "section", axis=0, tiled=True)
     down_all = lax.all_gather(w_down, "section", axis=0, tiled=True)
 
@@ -166,14 +172,14 @@
     def layer_forward(layer, inputs):
         onehot, chosen = tables(route_rows[layer], slot_rows[layer])
         normed_one, unit_one, inverse_one = norm_forward(
-            inputs, gain_all[layer, 0], shift_all[layer, 0]
+            inputs, gain_all[layer][0], shift_all[layer][0]
         )
         norm_one = normed_one.astype(half)
         qkv_rows = jnp.dot(norm_one, qkv_all[layer], preferred_element_type=jnp.float32).astype(half)
         attended, log_totals = attend_forward(qkv_rows, local_images)
         middle = inputs + jnp.dot(attended, out_all[layer], preferred_element_type=jnp.float32)
         normed_two, unit_two, inverse_two = norm_forward(
-            middle, gain_all[layer, 1], shift_all[layer, 1]
+            middle, gain_all[layer][1], shift_all[layer][1]
         )
         norm_two = normed_two.astype(half)
         logits = jnp.dot(norm_two, router_all[layer], preferred_element_type=jnp.float32)
@@ -237,10 +243,10 @@
             "te,de->td", d_logits, router_all[layer], preferred_element_type=jnp.float32
         )
         normed_two, unit_two, inverse_two = norm_forward(
-            middle, gain_all[layer, 1], shift_all[layer, 1]
+            middle, gain_all[layer][1], shift_all[layer][1]
         )
         d_middle_norm, gain_two, shift_two = norm_backward(
-            d_norm_two, unit_two, inverse_two, gain_all[layer, 1]
+            d_norm_two, unit_two, inverse_two, gain_all[layer][1]
         )
         d_middle = d_out + d_middle_norm
         d_middle_half = d_middle.astype(half)
@@ -252,10 +258,10 @@
             "te,de->td", d_qkv, qkv_all[layer], preferred_element_type=jnp.float32
         )
         normed_one, unit_one, inverse_one = norm_forward(
-            inputs, gain_all[layer, 0], shift_all[layer, 0]
+            inputs, gain_all[layer][0], shift_all[layer][0]
         )
         d_input_norm, gain_one, shift_one = norm_backward(
-            d_norm_one, unit_one, inverse_one, gain_all[layer, 0]
+            d_norm_one, unit_one, inverse_one, gain_all[layer][0]
         )
         d_input = d_middle + d_input_norm
         operands = [
@@ -278,6 +284,7 @@
     for layer in range(2):
         if layer > 0:
             stream = stream.astype(half).astype(jnp.float32)
+            gather_layer(lax.optimization_barrier((halves[1], saved_list[0][9]))[0])
         stream, saved = layer_forward(layer, stream)
         saved_list.append(saved)
     cotangent = edge_rows[1]

time: 866 us -> 920 us (1.062)
  waiting for transfers between devices: 400 us -> 456 us
  starting transfers between devices: 104 us -> 91.5 us
    all_gather x2 -> x4, waiting for transfers between devices: 91 us -> 116 us  [the longest x2 116 us: gather_layer(): part = lax.all_gather(shard[None], chips, axis=0, tiled=True)]
    all_gather x1, waiting for transfers between devices: 0.01 us -> 14.2 us  [on_device(): down_all = lax.all_gather(w_down, 'section', axis=0, tiled=True)]
    all_gather x1, waiting for transfers between devices: 0.02 us -> 14 us  [on_device(): up_all = lax.all_gather(w_up, 'section', axis=0, tiled=True)]
    all_to_all x4, starting transfers between devices: 29.5 us -> 18.5 us  [from_experts(): lax.all_to_all(chunks.transpose(1, 0, 2, 3), 'dp', split_axis=0, concat_a...]
  transfers between devices with their start and end apart: 36 -> 38, of which waited for: 19 -> 20; matrix products, arithmetic and copies ran while one was open for 21% -> 19% of each run, Pallas kernels for 0% -> 0%
where the time goes in v3:
time: 920 us; the launch traced here: 909 us
  waiting for transfers between devices  456 us (50%)
  matrix products  156 us (17%)
  starting transfers between devices  91.5 us (10%)
  other arithmetic  76.5 us (8%)
  local copies, waits for them, and re-layouts  63.5 us (7%)
  blocking collectives  49.5 us (5%)
  between operations  16.3 us (2%)
    all_gather x4, waiting for transfers between devices, to_experts(): return lax.all_gather(arrived, 'dp', axis=1, tiled=True)  144 us
    all_to_all x4, waiting for transfers between devices, from_experts(): lax.all_to_all(chunks.transpose(1, 0, 2, 3), 'dp', split_axis=0, concat_a...  122 us
    all_gather x2, waiting for transfers between devices, gather_layer(): part = lax.all_gather(shard[None], chips, axis=0, tiled=True)  116 us
    all_to_all x4, blocking collectives, to_experts(): lax.all_to_all(blocks, 'expert', split_axis=0, concat_axis=1, tiled=True)  41.9 us
    convert_element_type x2, other arithmetic, layer_forward(): hidden = jax.nn.gelu(pre_act, approximate=False).astype(half)  20.2 us
    all_to_all x4, starting transfers between devices, from_experts(): lax.all_to_all(chunks.transpose(1, 0, 2, 3), 'dp', split_axis=0, concat_a...  18.5 us
  transfers between devices with their start and end apart: 38, of which 20 were waited for; matrix products, arithmetic and copies ran while one was open for 19% of the time, Pallas kernels for 0%

profile of v3, /device:TPU:0, one launch (start us, length us, event | category | flops | bytes accessed | tf_op | source)
XLA Modules:
  0.0 908.6 jit_solution(2004760036980411608)
XLA Ops:
  14.8 65.8 %all-gather.14.cloned.1.call-done = bf16[16,24,3200]{2,1,0:T(8,128)(2,1)} async-done(((bf16[1,24,3200]{2,1,0:T(8,128)(2,1)}), bf16[16,24,3200]{2,1,0:T(8,128)(2,1)}) %all-gather.14.cloned.1.call-update) | async-done | bytes 2457616 | tf_op jit(solution)/shard_map/all_gather | solution.py:134
  111.3 11.7 %all_to_all.144 = bf16[8,40,768]{2,1,0:T(8,128)(2,1)S(1)} all-to-all(bf16[8,40,768]{2,1,0:T(8,128)(2,1)S(1)} %bitcast.359), channel_id=1, replica_groups=mesh['section'=2,'dp'=4,'expert'=4] {'expert'}, dimensions={0} | all-to-all | bytes 983040 | tf_op jit(solution)/shard_map/all_to_all | solution.py:158
  124.5 41.5 %all-gather.16.cloned.1.call-done = bf16[2,640,768]{2,1,0:T(8,128)(2,1)} async-done(((bf16[2,160,768]{2,1,0:T(8,128)(2,1)}), bf16[2,640,768]{2,1,0:T(8,128)(2,1)}) %all-gather.16.cloned.1.call-update) | async-done | bytes 1966096 | tf_op jit(solution)/shard_map/all_gather | solution.py:159
  166.7 14.0 %all-gather.18.cloned.1.call-done = bf16[2,2,768,768]{3,2,1,0:T(8,128)(2,1)} async-done(((bf16[1,2,768,768]{3,2,1,0:T(8,128)(2,1)}), bf16[2,2,768,768]{3,2,1,0:T(8,128)(2,1)}) %all-gather.18.cloned.1.call-update) | async-done | bytes 4718608 | tf_op jit(solution)/shard_map/all_gather | solution.py:144
  187.5 9.8 %fusion.6 = bf16[2,640,768]{2,1,0:T(8,128)(2,1)} fusion(f32[2,640,768]{2,1,0:T(8,128)S(1)} %get-tuple-element.112, u8[640,768]{1,0:T(8,128)(4,1)S(1)} %get-tuple-element.53, u8[640,768]{1,0:T(8,128)(4,1)S(1)} %get-tuple-element.52), kind=kLoop, calls=%fused_computation.13 | loop fusion | flops 68812800 | bytes 6881280 | tf_op jit(solution)/shard_map/convert_element_type | solution.py:196
  197.3 50.0 %all-gather.30.cloned.1.call-done = bf16[384,3200]{1,0:T(8,128)(2,1)} async-done(((bf16[24,3200]{1,0:T(8,128)(2,1)}), bf16[384,3200]{1,0:T(8,128)(2,1)}) %all-gather.30.cloned.1.call-update) | async-done | bytes 2457616 | tf_op jit(solution)/shard_map/all_gather | solution.py:134
  247.4 14.2 %all-gather.20.cloned.1.call-done = bf16[2,2,768,768]{3,2,1,0:T(8,128)(2,1)} async-done(((bf16[1,2,768,768]{3,2,1,0:T(8,128)(2,1)}), bf16[2,2,768,768]{3,2,1,0:T(8,128)(2,1)}) %all-gather.20.cloned.1.call-update) | async-done | bytes 4718608 | tf_op jit(solution)/shard_map/all_gather | solution.py:145
  273.8 44.1 %all-to-all-done.5 = bf16[4,2,160,768]{3,2,1,0:T(8,128)(2,1)} async-done(((bf16[4,2,160,768]{3,2,1,0:T(8,128)(2,1)}), bf16[4,2,160,768]{3,2,1,0:T(8,128)(2,1)}, u32[]{:S(2)}, u32[]{:S(2)}) %all-to-all-start.5) | async-done | bytes 1966112 | tf_op jit(solution)/shard_map/all_to_all | solution.py:163
  355.5 9.6 %all_to_all.145 = bf16[8,40,768]{2,1,0:T(8,128)(2,1)S(1)} all-to-all(bf16[8,40,768]{2,1,0:T(8,128)(2,1)S(1)} %bitcast.360), channel_id=1, replica_groups=mesh['section'=2,'dp'=4,'expert'=4] {'expert'}, dimensions={0} | all-to-all | bytes 983040 | tf_op jit(solution)/shard_map/all_to_all | solution.py:158
  370.1 9.6 %all_to_all.146 = bf16[8,40,768]{2,1,0:T(8,128)(2,1)S(1)} all-to-all(bf16[8,40,768]{2,1,0:T(8,128)(2,1)S(1)} %bitcast.406), channel_id=1, replica_groups=mesh['section'=2,'dp'=4,'expert'=4] {'expert'}, dimensions={0} | all-to-all | bytes 983040 | tf_op jit(solution)/shard_map/all_to_all | solution.py:158
  380.5 26.5 %all-gather.24.cloned.1.call-done = bf16[2,640,768]{2,1,0:T(8,128)(2,1)} async-done(((bf16[2,160,768]{2,1,0:T(8,128)(2,1)}), bf16[2,640,768]{2,1,0:T(8,128)(2,1)}) %all-gather.24.cloned.1.call-update) | async-done | bytes 1966096 | tf_op jit(solution)/shard_map/all_gather | solution.py:159
  407.0 7.8 fusion.108
  414.8 36.2 %all-gather.22.cloned.1.call-done = bf16[2,640,768]{2,1,0:T(8,128)(2,1)} async-done(((bf16[2,160,768]{2,1,0:T(8,128)(2,1)}), bf16[2,640,768]{2,1,0:T(8,128)(2,1)}) %all-gather.22.cloned.1.call-update) | async-done | bytes 1966096 | tf_op jit(solution)/shard_map/all_gather | solution.py:159
  466.4 10.3 %fusion.15 = bf16[2,640,768]{2,1,0:T(8,128)(2,1)S(1)} fusion(f32[2,640,768]{2,1,0:T(8,128)} %get-tuple-element.117, u8[640,768]{1,0:T(8,128)(4,1)} %get-tuple-element.51, u8[640,768]{1,0:T(8,128)(4,1)} %get-tuple-element.50), kind=kLoop, calls=%fused_computation.22 | loop fusion | flops 68812800 | bytes 6881280 | tf_op jit(solution)/shard_map/convert_element_type | solution.py:196
  482.2 29.7 %all-to-all-done.9 = bf16[4,2,160,768]{3,2,1,0:T(8,128)(2,1)} async-done(((bf16[4,2,160,768]{3,2,1,0:T(8,128)(2,1)}), bf16[4,2,160,768]{3,2,1,0:T(8,128)(2,1)}, u32[]{:S(2)}, u32[]{:S(2)}) %all-to-all-start.9) | async-done | bytes 1966112 | tf_op jit(solution)/shard_map/all_to_all | solution.py:163
  520.9 40.4 %all-to-all-done.11 = bf16[4,2,160,768]{3,2,1,0:T(8,128)(2,1)} async-done(((bf16[4,2,160,768]{3,2,1,0:T(8,128)(2,1)}), bf16[4,2,160,768]{3,2,1,0:T(8,128)(2,1)}, u32[]{:S(2)}, u32[]{:S(2)}) %all-to-all-start.11) | async-done | bytes 1966112 | tf_op jit(solution)/shard_map/all_to_all | solution.py:163
  621.2 10.9 %all_to_all.147 = bf16[8,40,768]{2,1,0:T(8,128)(2,1)S(1)} all-to-all(bf16[8,40,768]{2,1,0:T(8,128)(2,1)S(1)} %bitcast.405), channel_id=1, replica_groups=mesh['section'=2,'dp'=4,'expert'=4] {'expert'}, dimensions={0} | all-to-all | bytes 983040 | tf_op jit(solution)/shard_map/all_to_all | solution.py:158
  633.0 40.4 %all-gather.26.cloned.1.call-done = bf16[2,640,768]{2,1,0:T(8,128)(2,1)} async-done(((bf16[2,160,768]{2,1,0:T(8,128)(2,1)}), bf16[2,640,768]{2,1,0:T(8,128)(2,1)}) %all-gather.26.cloned.1.call-update) | async-done | bytes 1966096 | tf_op jit(solution)/shard_map/all_gather | solution.py:159
  726.6 7.7 all-to-all-done.14
  790.6 7.6 concatenate.94
  803.2 7.4 fusion.225
  845.3 13.6 %all-to-all-done.16 = bf16[4,4,48,3200]{3,2,1,0:T(8,128)(2,1)} async-done(((bf16[4,4,48,3200]{3,2,1,0:T(8,128)(2,1)}), bf16[4,4,48,3200]{3,2,1,0:T(8,128)(2,1)}, u32[]{:S(2)}, u32[]{:S(2)}) %all-to-all-start.16) | async-done | bytes 4915232 | tf_op jit(solution)/shard_map/all_to_all | solution.py:311
  867.0 8.6 select_bitcast_fusion.1
  886.3 11.2 %all-to-all-done.17 = bf16[4,48,3200]{2,1,0:T(8,128)(2,1)S(1)} async-done(((bf16[4,48,3200]{2,1,0:T(8,128)(2,1)}), bf16[4,48,3200]{2,1,0:T(8,128)(2,1)S(1)}, u32[]{:S(2)}, u32[]{:S(2)}) %all-to-all-start.17) | async-done | bytes 1228832 | tf_op jit(solution)/shard_map/all_to_all | solution.py:313
  (408 shorter events, 363.9 us)
Async XLA Ops:
  7.2 73.4 %all-gather.14.cloned.1.call-start = ((), (), s32[]{:S(2)}) async-start(), calls=%async_computation.18 | async-start | bytes 2611200 | tf_op jit(solution)/shard_map/all_gather | solution.py:134
  14.7 82.0 %all-gather.28.cloned.1.call-start = ((), (), s32[]{:S(2)}) async-start(), calls=%async_computation.25 | async-start | bytes 7372800 | tf_op jit(solution)/shard_map/all_gather | solution.py:135
  92.5 73.6 %all-gather.16.cloned.1.call-start = ((), (), s32[]{:S(2)}) async-start(), calls=%async_computation.19 | async-start | bytes 2457600 | tf_op jit(solution)/shard_map/all_gather | solution.py:159
  123.9 56.8 %all-gather.18.cloned.1.call-start = ((), (), s32[]{:S(2)}) async-start(), calls=%async_computation.20 | async-start | bytes 7077888 | tf_op jit(solution)/shard_map/all_gather | solution.py:144
  124.5 122.8 %all-gather.30.cloned.1.call-start = ((), (), s32[]{:S(2)}) async-start(), calls=%async_computation.26 | async-start | bytes 2611200 | tf_op jit(solution)/shard_map/all_gather | solution.py:134
  166.1 95.5 %all-gather.20.cloned.1.call-start = ((), (), s32[]{:S(2)}) async-start(), calls=%async_computation.21 | async-start | bytes 7077888 | tf_op jit(solution)/shard_map/all_gather | solution.py:145
  166.6 167.0 %all-gather.32.cloned.1.call-start = ((), (), s32[]{:S(2)}) async-start(), calls=%async_computation.27 | async-start | bytes 7372800 | tf_op jit(solution)/shard_map/all_gather | solution.py:135
  266.9 51.0 %all-to-all-start.5 = ((bf16[4,2,160,768]{3,2,1,0:T(8,128)(2,1)}), bf16[4,2,160,768]{3,2,1,0:T(8,128)(2,1)}, u32[]{:S(2)}, u32[]{:S(2)}) async-start(bf16[4,2,160,768]{3,2,1,0:T(8,128)(2,1)} %bitcast.335), calls=%async_computation.5 | async-start | bytes 3932160 | tf_op jit(solution)/shard_map/all_to_all | solution.py:163
  324.4 82.6 %all-gather.24.cloned.1.call-start = ((), (), s32[]{:S(2)}) async-start(), calls=%async_computation.23 | async-start | bytes 2457600 | tf_op jit(solution)/shard_map/all_gather | solution.py:159
  365.9 85.1 %all-gather.22.cloned.1.call-start = ((), (), s32[]{:S(2)}) async-start(), calls=%async_computation.22 | async-start | bytes 2457600 | tf_op jit(solution)/shard_map/all_gather | solution.py:159
  461.9 50.0 %all-to-all-start.9 = ((bf16[4,2,160,768]{3,2,1,0:T(8,128)(2,1)}), bf16[4,2,160,768]{3,2,1,0:T(8,128)(2,1)}, u32[]{:S(2)}, u32[]{:S(2)}) async-start(bf16[4,2,160,768]{3,2,1,0:T(8,128)(2,1)} %bitcast.337), calls=%async_computation.9 | async-start | bytes 3932160 | tf_op jit(solution)/shard_map/all_to_all | solution.py:163
  511.9 49.4 %all-to-all-start.11 = ((bf16[4,2,160,768]{3,2,1,0:T(8,128)(2,1)}), bf16[4,2,160,768]{3,2,1,0:T(8,128)(2,1)}, u32[]{:S(2)}, u32[]{:S(2)}) async-start(bf16[4,2,160,768]{3,2,1,0:T(8,128)(2,1)} %bitcast.336), calls=%async_computation.11 | async-start | bytes 3932160 | tf_op jit(solution)/shard_map/all_to_all | solution.py:163
  576.9 96.4 %all-gather.26.cloned.1.call-start = ((), (), s32[]{:S(2)}) async-start(), calls=%async_computation.24 | async-start | bytes 2457600 | tf_op jit(solution)/shard_map/all_gather | solution.py:159
  684.2 50.1 %all-to-all-start.14 = ((bf16[4,2,160,768]{3,2,1,0:T(8,128)(2,1)}), bf16[4,2,160,768]{3,2,1,0:T(8,128)(2,1)}, u32[]{:S(2)}, u32[]{:S(2)}) async-start(bf16[4,2,160,768]{3,2,1,0:T(8,128)(2,1)} %bitcast.334), calls=%async_computation.14 | async-start | bytes 3932160 | tf_op jit(solution)/shard_map/all_to_all | solution.py:163
  711.7 71.3 %collective-permute-start.9 = (bf16[197,768]{1,0:T(8,128)(2,1)}, bf16[197,768]{1,0:T(8,128)(2,1)}, u32[]{:S(2)}, u32[]{:S(2)}) collective-permute-start(bf16[197,768]{1,0:T(8,128)(2,1)} %copy-done.30), channel_id=1, source_target_pairs={{0,16},{1,17},{2,18},{3,19},{4,20},{5,21},{6,22},{7,23},{8,24},{9,... | collective-permute-start | bytes 907784 | tf_op jit(solution)/shard_map/ppermute | solution.py:268
  715.9 69.1 %collective-permute-start.5 = (bf16[197,2304]{1,0:T(8,128)(2,1)}, bf16[197,2304]{1,0:T(8,128)(2,1)}, u32[]{:S(2)}, u32[]{:S(2)}) collective-permute-start(bf16[197,2304]{1,0:T(8,128)(2,1)} %pad_maximum_fusion), channel_id=1, source_target_pairs={{0,16},{1,17},{2,18},{3,19},{4,20},{5,21},{6,22},{7,23},{8,24},{9,... | collective-permute-start | bytes 2723336 | tf_op jit(solution)/shard_map/ppermute | solution.py:268
  723.1 53.9 %collective-permute-start.11 = (f32[12,768]{1,0:T(8,128)S(1)}, f32[12,768]{1,0:T(8,128)}, u32[]{:S(2)}, u32[]{:S(2)}) collective-permute-start(f32[12,768]{1,0:T(8,128)S(1)} %concatenate.92), channel_id=1, source_target_pairs={{0,16},{1,17},{2,18},{3,19},{4,20},{5,21},{6,22},{7,23},{8,24},{9,... | collective-permute-start | bytes 110600 | tf_op jit(solution)/shard_map/ppermute | solution.py:278
  798.2 60.7 %all-to-all-start.16 = ((bf16[4,4,48,3200]{3,2,1,0:T(8,128)(2,1)}), bf16[4,4,48,3200]{3,2,1,0:T(8,128)(2,1)}, u32[]{:S(2)}, u32[]{:S(2)}) async-start(bf16[4,4,48,3200]{3,2,1,0:T(8,128)(2,1)} %bitcast.329), calls=%async_computation.16 | async-start | bytes 9830400 | tf_op jit(solution)/shard_map/all_to_all | solution.py:311
  810.6 56.3 %collective-permute-start.13 = (bf16[2,768,768]{2,1,0:T(8,128)(2,1)}, bf16[2,768,768]{2,1,0:T(8,128)(2,1)}, u32[]{:S(2)}, u32[]{:S(2)}) collective-permute-start(bf16[2,768,768]{2,1,0:T(8,128)(2,1)} %get-tuple-element.124), channel_id=1, source_target_pairs={{0,16},{1,17},{2,18},{3,19},{4,20},{5,21},{6,22},{7,23},{8,24},{9,... | collective-permute-start | bytes 7077896 | tf_op jit(solution)/shard_map/ppermute | solution.py:239
  821.0 45.9 %collective-permute-start.12 = (bf16[2,768,768]{2,1,0:T(8,128)(2,1)}, bf16[2,768,768]{2,1,0:T(8,128)(2,1)}, u32[]{:S(2)}, u32[]{:S(2)}) collective-permute-start(bf16[2,768,768]{2,1,0:T(8,128)(2,1)} %get-tuple-element.126), channel_id=1, source_target_pairs={{16,0},{17,1},{18,2},{19,3},{20,4},{21,5},{22,6},{23,7},{24,8},{25... | collective-permute-start | bytes 7077896 | tf_op jit(solution)/shard_map/ppermute | solution.py:239
  827.6 49.5 %collective-permute-start.15 = (bf16[2,768,768]{2,1,0:T(8,128)(2,1)}, bf16[2,768,768]{2,1,0:T(8,128)(2,1)}, u32[]{:S(2)}, u32[]{:S(2)}) collective-permute-start(bf16[2,768,768]{2,1,0:T(8,128)(2,1)} %get-tuple-element.128), channel_id=1, source_target_pairs={{0,16},{1,17},{2,18},{3,19},{4,20},{5,21},{6,22},{7,23},{8,24},{9,... | collective-permute-start | bytes 7077896 | tf_op jit(solution)/shard_map/ppermute | solution.py:240
  838.8 38.4 %collective-permute-start.14 = (bf16[2,768,768]{2,1,0:T(8,128)(2,1)}, bf16[2,768,768]{2,1,0:T(8,128)(2,1)}, u32[]{:S(2)}, u32[]{:S(2)}) collective-permute-start(bf16[2,768,768]{2,1,0:T(8,128)(2,1)} %get-tuple-element.130), channel_id=1, source_target_pairs={{16,0},{17,1},{18,2},{19,3},{20,4},{21,5},{22,6},{23,7},{24,8},{25... | collective-permute-start | bytes 7077896 | tf_op jit(solution)/shard_map/ppermute | solution.py:240
  840.0 42.6 %collective-permute-start.1 = (f32[197,768]{1,0:T(8,128)}, f32[197,768]{1,0:T(8,128)}, u32[]{:S(2)}, u32[]{:S(2)}) collective-permute-start(f32[197,768]{1,0:T(8,128)} %get-tuple-element.101), channel_id=1, source_target_pairs={{0,16},{1,17},{2,18},{3,19},{4,20},{5,21},{6,22},{7,23},{8,24},{9,... | collective-permute-start | bytes 1815560 | tf_op jit(solution)/shard_map/ppermute | solution.py:324
  863.4 34.2 %all-to-all-start.17 = ((bf16[4,48,3200]{2,1,0:T(8,128)(2,1)}), bf16[4,48,3200]{2,1,0:T(8,128)(2,1)S(1)}, u32[]{:S(2)}, u32[]{:S(2)}) async-start(bf16[4,48,3200]{2,1,0:T(8,128)(2,1)} %reduce_sum.473), calls=%async_computation.17 | async-start | bytes 2457600 | tf_op jit(solution)/shard_map/all_to_all | solution.py:313
  (89 other events, 1272.5 us)
Sparse Core Ops, SparseCore 0:
  14.8 65.6 all-gather.13
  82.1 13.9 all-gather.27
  124.0 41.9 all-gather.15
  167.4 13.2 all-gather.17
  183.3 64.0 all-gather.29
  248.7 12.7 all-gather.19
  263.1 15.8 all-gather.31
  366.0 40.9 all-gather.23
  408.6 42.3 all-gather.21
  633.1 40.1 all-gather.25
